TPU v7x, 32 devices: a whole 2x2x4 slice. The times are simulated.
32 devices in a mesh: row: 4 (over z), col: 8 (over y, x, core).
Axes of the slice: x: 2, y: 2, z: 4, core: 2. Of those that a mesh axis runs over, the one named last changes fastest.
Arguments:
- trailing: float32 [20480, 20480], P('row', 'col'), may hold values from -24 to 24
- panel_block: float32 [20480, 128], P(('row', 'col')), may hold values from -0.2795085 to 0.2795085
Outputs:
- trailing_out: float32 [20480, 20480], P('row', 'col')
- r_factor: float32 [128, 128], replicated
- first_factor: float32 [128, 128], replicated
All inputs are finite; a program needn't handle non-finite values.
Results may differ from a plain program's by a relative error of at most 0.0003.
Values sent between devices are 32-bit elements; how exact they have to be, the bound alone decides.
No kernel may reach another device: no remote copies, remote signals or barrier semaphores. Data moves between devices by JAX's collectives and lax.ppermute only.
A program may use at most 192 MiB of HBM per device.

v0:
```python
import jax
import jax.numpy as jnp
from jax import lax
from jax.sharding import PartitionSpec as P

HIGHEST = lax.Precision.HIGHEST


def broadcast(block, axis, holder):
    block = jnp.where(lax.axis_index(axis) == holder, block, jnp.zeros_like(block))
    return lax.psum(block, axis)


def matmul(first, second):
    return jnp.dot(first, second, preferred_element_type=jnp.float32, precision=HIGHEST)


def column_block(block_rows, col_width, my_column, per_owner):
    wanted = lax.dynamic_slice_in_dim(block_rows, my_column % per_owner * col_width, col_width, 0)
    return broadcast(wanted, "row", my_column // per_owner)


def on_device(trailing, panel_block):
    row_devices = lax.axis_size("row")
    col_devices = lax.axis_size("col")
    per_owner = col_devices // row_devices
    col_width = trailing.shape[1]
    my_column = lax.axis_index("col")
    gram_one = lax.psum(matmul(panel_block.T, panel_block), ("row", "col"))
    low_one = jnp.linalg.cholesky(gram_one)
    first_q = lax.linalg.triangular_solve(
        low_one, panel_block, left_side=False, lower=True, transpose_a=True
    )
    gram_two = lax.psum(matmul(first_q.T, first_q), ("row", "col"))
    low_two = jnp.linalg.cholesky(gram_two)
    ortho_basis = lax.linalg.triangular_solve(
        low_two, first_q, left_side=False, lower=True, transpose_a=True
    )
    r_factor = matmul(low_two.T, low_one.T)
    basis_block = lax.all_gather(ortho_basis, "col", axis=0, tiled=True)
    basis_cols = column_block(basis_block, col_width, my_column, per_owner)
    products = lax.psum_scatter(
        matmul(trailing, basis_cols), "col", scatter_dimension=0, tiled=True
    )
    projected = lax.psum(matmul(ortho_basis.T, products), ("row", "col"))
    correction = 2.0 * (products - matmul(ortho_basis, projected))
    correction_rows = lax.all_gather(correction, "col", axis=0, tiled=True)
    correction_cols = column_block(correction_rows, col_width, my_column, per_owner)
    left_factor = jnp.concatenate([basis_block, correction_rows], axis=1)
    right_factor = jnp.concatenate([correction_cols, basis_cols], axis=1)
    trailing_out = trailing - matmul(left_factor, right_factor.T)
    return (trailing_out, r_factor, low_one.T)


def solution(mesh):
    in_specs = (P("row", "col"), P(("row", "col"), None))
    out_specs = (P("row", "col"), P(), P())
    return jax.shard_map(
        on_device, mesh=mesh, in_specs=in_specs, out_specs=out_specs, check_vma=False
    )
```

profile of v0, /device:TPU:0, one launch (start us, length us, event | category | flops | bytes accessed | tf_op | source)
XLA Modules:
  0.0 787.1 jit_solution(7211402984523211632)
XLA Ops:
  7.2 0.9 copy-done
  8.1 1.3 fusion.28
  9.5 126.7 %all-reduce.6.cloned.1.call-done = f32[128,128]{0,1:T(8,128)} async-done(((f32[128,128]{0,1:T(8,128)}), f32[128,128]{0,1:T(8,128)}) %all-reduce.6.cloned.1.call-update) | async-done | bytes 65552 | tf_op jit(solution)/shard_map/psum | solution.py:29
  136.3 0.9 copy.6
  137.2 0.9 fusion.10
  138.1 11.7 %cholesky.44 = f32[128,128]{1,0:T(8,128)S(1)} custom-call(f32[128,128]{1,0:T(8,128)S(1)} %fusion.10), custom_call_target="Cholesky" | custom-call | tf_op jit(solution)/shard_map/jit(cholesky)/cholesky | solution.py:30
  149.8 0.7 compare_reduce_fusion.1
  151.2 9.8 %custom-call.6 = f32[1,128,128]{1,2,0:T(8,128)S(1)} custom-call(f32[1,128,128]{2,1,0:T(8,128)S(1)} %get-tuple-element.9), custom_call_target="InvertDiagBlocksLowerTriangular" | custom-call | tf_op jit(solution)/shard_map/triangular_solve/custom-call.0 | solution.py:31
  161.5 1.1 fusion.29
  162.8 120.6 %all-reduce.8.cloned.1.call-done = f32[128,128]{0,1:T(8,128)} async-done(((f32[128,128]{0,1:T(8,128)}), f32[128,128]{0,1:T(8,128)}) %all-reduce.8.cloned.1.call-update) | async-done | bytes 65552 | tf_op jit(solution)/shard_map/psum | solution.py:34
  283.4 0.9 copy.8
  284.3 0.9 fusion.8
  285.2 11.7 %cholesky.55 = f32[128,128]{1,0:T(8,128)S(1)} custom-call(f32[128,128]{1,0:T(8,128)S(1)} %fusion.8), custom_call_target="Cholesky" | custom-call | tf_op jit(solution)/shard_map/jit(cholesky)/cholesky | solution.py:35
  296.9 0.7 compare_reduce_fusion
  297.6 0.6 select_bitcast_fusion
  298.2 9.8 %custom-call.7 = f32[1,128,128]{1,2,0:T(8,128)S(1)} custom-call(f32[1,128,128]{2,1,0:T(8,128)S(1)} %select_bitcast_fusion), custom_call_target="InvertDiagBlocksLowerTriangular" | custom-call | tf_op jit(solution)/shard_map/triangular_solve/custom-call.0 | solution.py:36
  308.1 1.2 convolution_bitcast_fusion.1
  309.4 31.3 %all-gather.3.cloned.1.call-done = f32[5120,128]{0,1:T(8,128)} async-done(((f32[640,128]{0,1:T(8,128)}), f32[5120,128]{0,1:T(8,128)}) %all-gather.3.cloned.1.call-update) | async-done | bytes 2621456 | tf_op jit(solution)/shard_map/all_gather | solution.py:40
  340.6 2.5 dynamic-slice_select_fusion.1
  343.4 60.1 %all-reduce.10.cloned.1.call-done = f32[2560,128]{0,1:T(8,128)} async-done(((f32[2560,128]{0,1:T(8,128)}), f32[2560,128]{0,1:T(8,128)}) %all-reduce.10.cloned.1.call-update) | async-done | bytes 1310736 | tf_op jit(solution)/shard_map/psum | solution.py:11
  403.5 59.0 %convolution_bitcast_fusion = f32[5120,128]{0,1:T(8,128)} fusion(f32[2560,128]{0,1:T(8,128)} %all-reduce.10.cloned.1.call-done, f32[5120,2560]{1,0:T(8,128)} %param.5), kind=kOutput, calls=%fused_computation.1 | convolution fusion | flops 20132659200 | bytes 56360960 | tf_op jit(solution)/shard_map/dot_general | solution.py:15
  462.6 43.2 %reduce-scatter.2.cloned.1.call-done = f32[640,128]{0,1:T(8,128)} async-done(((f32[5120,128]{0,1:T(8,128)}), f32[640,128]{0,1:T(8,128)}) %reduce-scatter.2.cloned.1.call-update) | async-done | bytes 327696 | tf_op jit(solution)/shard_map/reduce_scatter | solution.py:42
  505.8 2.1 fusion.30
  508.0 123.2 %all-reduce.12.cloned.1.call-done = f32[128,128]{1,0:T(8,128)} async-done(((f32[128,128]{1,0:T(8,128)}), f32[128,128]{1,0:T(8,128)}) %all-reduce.12.cloned.1.call-update) | async-done | bytes 65552 | tf_op jit(solution)/shard_map/psum | solution.py:45
  631.2 2.2 fusion.6
  633.7 31.2 %all-gather.5.cloned.1.call-done = f32[5120,128]{0,1:T(8,128)} async-done(((f32[640,128]{0,1:T(8,128)}), f32[5120,128]{0,1:T(8,128)}) %all-gather.5.cloned.1.call-update) | async-done | bytes 2621456 | tf_op jit(solution)/shard_map/all_gather | solution.py:47
  664.9 2.5 dynamic-slice_select_fusion
  667.4 0.7 copy.10
  668.1 2.2 fusion.17
  670.3 57.7 %all-reduce.14.cloned.1.call-done = f32[2560,128]{0,1:T(8,128)} async-done(((f32[2560,128]{0,1:T(8,128)}), f32[2560,128]{0,1:T(8,128)}) %all-reduce.14.cloned.1.call-update) | async-done | bytes 1310736 | tf_op jit(solution)/shard_map/psum | solution.py:11
  728.0 1.5 fusion.49
  729.5 50.8 %convolution_subtract_fusion = f32[5120,2560]{1,0:T(8,128)} fusion(f32[5120,2560]{1,0:T(8,128)} %param.5, f32[5120,128]{0,1:T(8,128)} %all-gather.5.cloned.1.call-done, f32[5120,128]{0,1:T(8,128)} %all-gather.3.cloned.1.call-done, f32[2560,256]{0,1:T(8,128)S(1)} %fusion.49), kind=kOutput, calls=%fused_computation | convolution fusion | flops 40279736320 | bytes 112721920 | tf_op jit(solution)/shard_map/dot_general | solution.py:15
  (27 shorter events, 2.4 us)
Async XLA Ops:
  7.2 1.0 copy-start
  7.2 129.1 %all-reduce.6.cloned.1.call-start = ((), (), s32[]{:S(2)}) async-start(), calls=%async_computation.1 | async-start | bytes 131072 | tf_op jit(solution)/shard_map/psum | solution.py:29
  9.5 273.9 %all-reduce.8.cloned.1.call-start = ((), (), s32[]{:S(2)}) async-start(), calls=%async_computation.2 | async-start | bytes 131072 | tf_op jit(solution)/shard_map/psum | solution.py:34
  162.6 178.0 %all-gather.3.cloned.1.call-start = ((), (), s32[]{:S(2)}) async-start(), calls=%async_computation.3 | async-start | bytes 2949120 | tf_op jit(solution)/shard_map/all_gather | solution.py:40
  309.3 94.3 %all-reduce.10.cloned.1.call-start = ((), (), s32[]{:S(2)}) async-start(), calls=%async_computation.4 | async-start | bytes 2621440 | tf_op jit(solution)/shard_map/psum | solution.py:11
  343.1 162.7 %reduce-scatter.2.cloned.1.call-start = ((), (), s32[]{:S(2)}) async-start(), calls=%async_computation.5 | async-start | bytes 2949120 | tf_op jit(solution)/shard_map/reduce_scatter | solution.py:42
  462.6 43.2 %copy-start.3 = (f32[640,128]{0,1:T(8,128)S(1)}, f32[640,128]{0,1:T(8,128)}, u32[]{:S(2)}) copy-start(f32[640,128]{0,1:T(8,128)} %convolution_bitcast_fusion.1) | copy-start | bytes 983044
  462.6 168.6 %all-reduce.12.cloned.1.call-start = ((), (), s32[]{:S(2)}) async-start(), calls=%async_computation.6 | async-start | bytes 131072 | tf_op jit(solution)/shard_map/psum | solution.py:45
  507.9 220.0 %copy-start.2 = (f32[2560,128]{0,1:T(8,128)S(1)}, f32[2560,128]{0,1:T(8,128)}, u32[]{:S(2)}) copy-start(f32[2560,128]{0,1:T(8,128)} %all-reduce.10.cloned.1.call-done) | copy-start | bytes 3932164
  507.9 157.0 %all-gather.5.cloned.1.call-start = ((), (), s32[]{:S(2)}) async-start(), calls=%async_computation.7 | async-start | bytes 2949120 | tf_op jit(solution)/shard_map/all_gather | solution.py:47
  633.4 94.5 %all-reduce.14.cloned.1.call-start = ((), (), s32[]{:S(2)}) async-start(), calls=%async_computation.8 | async-start | bytes 2621440 | tf_op jit(solution)/shard_map/psum | solution.py:11
  729.5 50.8 %copy-start.1 = (f32[640,128]{1,0:T(8,128)S(1)}, f32[640,128]{1,0:T(8,128)}, u32[]{:S(2)}) copy-start(f32[640,128]{1,0:T(8,128)} %param.6) | copy-start | bytes 983044
Sparse Core Ops, SparseCore 0:
  14.1 122.0 all-reduce.5
  162.7 120.6 all-reduce.7
  309.4 31.1 all-gather.2
  343.4 60.0 all-reduce.9
  462.7 43.0 reduce-scatter.1
  511.8 119.3 all-reduce.11
  633.7 31.1 all-gather.4
  667.9 60.0 all-reduce.13
where the time goes:
time: 788 us; the launch traced here: 787 us
  waiting for transfers between devices  594 us (75%)
  matrix products  120 us (15%)
  other arithmetic  53.9 us (7%)
  between operations  14.3 us (2%)
    psum x1, waiting for transfers between devices, on_device(): gram_one = lax.psum(matmul(panel_block.T, panel_block), ('row', 'col'))  127 us
    psum x1, waiting for transfers between devices, on_device(): projected = lax.psum(matmul(ortho_basis.T, products), ('row', 'col'))  123 us
    psum x1, waiting for transfers between devices, on_device(): gram_two = lax.psum(matmul(first_q.T, first_q), ('row', 'col'))  121 us
    dot_general x7, matrix products, matmul(): jnp.dot(first, second, preferred_element_type=jnp.float32, precision=HIGH...  119 us
    psum x2, waiting for transfers between devices, broadcast(): return lax.psum(block, axis)  118 us
    reduce_scatter x1, waiting for transfers between devices, on_device(): lax.psum_scatter(matmul(trailing, basis_cols), 'col', scatter_dimension=0...  43.2 us
    all_gather x1, waiting for transfers between devices, on_device(): basis_block = lax.all_gather(ortho_basis, 'col', axis=0, tiled=True)  31.3 us
    all_gather x1, waiting for transfers between devices, on_device(): correction_rows = lax.all_gather(correction, 'col', axis=0, tiled=True)  31.2 us
  transfers between devices with their start and end apart: 8, of which 8 were waited for; matrix products, arithmetic and copies ran while one was open for 0% of the time, Pallas kernels for 0%

commit v1 on v0

v1 whole, which is shorter than its diff:
```python
import functools

import jax
import jax.numpy as jnp
from jax import lax
from jax.experimental import pallas as pl
from jax.experimental.pallas import tpu as pltpu
from jax.sharding import PartitionSpec as P


HIGHEST = lax.Precision.HIGHEST
F32 = jnp.float32
BF16 = jnp.bfloat16
PRODUCT_GROUPS = ((0, 1, 2), (3,))
UPDATE_GROUPS = ((0, 1), (2, 3))
BUFFERS = 4
VMEM_LIMIT = 60 * 1024 * 1024


def matmul(first, second):
    return jnp.dot(first, second, preferred_element_type=F32, precision=HIGHEST)


def split(block):
    high = block.astype(BF16)
    return high, (block - high.astype(F32)).astype(BF16)


def contract(first, second, dims):
    return lax.dot_general(first, second, (dims, ((), ())), preferred_element_type=F32)


def factor_kernel(gram_ref, upper_ref, inverse_ref):
    order = gram_ref.shape[0]
    step = 8
    lane = lax.broadcasted_iota(jnp.int32, (1, order), 1)
    left = gram_ref[...]
    row_id = lax.broadcasted_iota(jnp.int32, (order, order), 0)
    right = (row_id == lax.broadcasted_iota(jnp.int32, (order, order), 1)).astype(F32)
    for base in range(0, order, step):
        rows_l = [left[base + i:base + i + 1, :] for i in range(step)]
        rows_r = [right[base + i:base + i + 1, :] for i in range(step)]
        pivots = [
            [jnp.broadcast_to(rows_l[i][:, base + j:base + j + 1], (1, order)) for j in range(step)]
            for i in range(step)
        ]
        columns = [
            jnp.broadcast_to(left[:, base + j:base + j + 1], (order, order)) for j in range(step)
        ]
        for j in range(step):
            pivot = pivots[j][j]
            root = lax.rsqrt(pivot)
            root = root * (1.5 - 0.5 * pivot * root * root)
            recip = root * root
            upper_ref[base + j:base + j + 1, :] = jnp.where(lane >= base + j, rows_l[j] * root, 0.0)
            inverse_ref[base + j:base + j + 1, :] = rows_r[j] * root
            for i in range(j + 1, step):
                ratio = pivots[j][i] * recip
                rows_l[i] = rows_l[i] - ratio * rows_l[j]
                rows_r[i] = rows_r[i] - ratio * rows_r[j]
                for k in range(i, step):
                    pivots[i][k] = pivots[i][k] - ratio * pivots[j][k]
                columns[i] = columns[i] - columns[j] * ratio
            if base + step < order:
                scaled = columns[j] * recip
                left = left - scaled * rows_l[j]
                right = right - scaled * rows_r[j]


def factor(gram):
    return pl.pallas_call(
        factor_kernel,
        out_shape=[jax.ShapeDtypeStruct(gram.shape, F32)] * 2,
        name="factor",
    )(gram)


def contract_split(first, second, dims):
    out = contract(first[0], second[0], dims)
    out = out + contract(first[0], second[1], dims)
    return out + contract(first[1], second[0], dims)


def blocking(rows, count):
    sub = 2 if rows % 16 == 0 and count > 1 else 1
    return sub, rows // sub


def product_kernel(count, has_start, *refs):
    (cols_ref, order_ref, trailing_ref), refs = refs[:3], refs[3:]
    basis_refs, refs = refs[:count], refs[count:]
    if has_start:
        start_ref, refs = refs[0], refs[1:]
    out_ref, split_ref, buffer_ref, before_ref, result_ref, in_sems, out_sems = refs
    buffers, block, _ = buffer_ref.shape
    piece, width = basis_refs[0].shape
    height = out_ref.shape[0]
    pieces = order_ref.shape[0]
    rows = height // pieces
    sub = rows // block
    steps = height // block

    def window(step):
        return pl.ds(pl.multiple_of(step * block, 8), block)

    def in_copies(step):
        slot = lax.rem(step, buffers)
        top = order_ref[step // sub] * rows + lax.rem(step, sub) * block
        top = pl.multiple_of(top, 8)
        out = []
        for i in range(count):
            left = cols_ref[i] * piece
            if piece % 128 == 0:
                left = pl.multiple_of(left, 128)
            source = trailing_ref.at[pl.ds(top, block), pl.ds(left, piece)]
            target = buffer_ref.at[slot, :, pl.ds(i * piece, piece)]
            out.append(pltpu.make_async_copy(source, target, in_sems.at[slot, i]))
        if has_start:
            source = start_ref.at[window(step), :]
            out.append(pltpu.make_async_copy(source, before_ref.at[slot], in_sems.at[slot, count]))
        return out

    def out_copy(step):
        slot = lax.rem(step, buffers)
        return pltpu.make_async_copy(result_ref.at[slot], out_ref.at[window(step), :], out_sems.at[slot])

    for step in range(min(buffers - 1, steps)):
        for copy in in_copies(jnp.int32(step)):
            copy.start()
    for i, basis_ref in enumerate(basis_refs):
        high, low = split(basis_ref[...])
        split_ref[i * piece:(i + 1) * piece, :width] = high
        split_ref[i * piece:(i + 1) * piece, width:] = low

    def body(step, carry):
        @pl.when(step + buffers - 1 < steps)
        def _():
            for copy in in_copies(step + buffers - 1):
                copy.start()

        for copy in in_copies(step):
            copy.wait()

        @pl.when(step >= buffers)
        def _():
            out_copy(step - buffers).wait()

        slot = lax.rem(step, buffers)
        high, low = split(buffer_ref[slot])
        both = contract(high, split_ref[...], ((1,), (0,)))
        small = contract(low, split_ref[:, :width], ((1,), (0,)))
        total = both[:, :width] + both[:, width:] + small
        if has_start:
            total = total + before_ref[slot]
        result_ref[slot] = total
        out_copy(step).start()
        return carry

    lax.fori_loop(0, steps, body, 0)
    for step in range(max(steps - buffers, 0), steps):
        out_copy(jnp.int32(step)).wait()


def product(trailing, basis, columns, order, start):
    height = trailing.shape[0]
    count = len(basis)
    piece, width = basis[0].shape
    _, block = blocking(height // order.shape[0], count)
    args = [columns, order, trailing, *basis]
    smem = pl.BlockSpec(memory_space=pltpu.SMEM)
    vmem = pl.BlockSpec(memory_space=pltpu.VMEM)
    hbm = pl.BlockSpec(memory_space=pl.ANY)
    in_specs = [smem, smem, hbm] + [vmem] * count
    if start is not None:
        args.append(start)
        in_specs.append(hbm)
    return pl.pallas_call(
        functools.partial(product_kernel, count, start is not None),
        in_specs=in_specs,
        out_specs=hbm,
        out_shape=jax.ShapeDtypeStruct((height, width), F32),
        scratch_shapes=[
            pltpu.VMEM((count * piece, 2 * width), BF16),
            pltpu.VMEM((BUFFERS, block, count * piece), F32),
            pltpu.VMEM((BUFFERS, block, width), F32),
            pltpu.VMEM((BUFFERS, block, width), F32),
            pltpu.SemaphoreType.DMA((BUFFERS, count + 1)),
            pltpu.SemaphoreType.DMA((BUFFERS,)),
        ],
        compiler_params=pltpu.CompilerParams(vmem_limit_bytes=VMEM_LIMIT),
        name="product",
    )(*args)


def update_kernel(count, has_start, *refs):
    (cols_ref, order_ref, trailing_ref, left_a_ref, left_b_ref), refs = refs[:5], refs[5:]
    right_a_refs, refs = refs[:count], refs[count:]
    right_b_refs, refs = refs[:count], refs[count:]
    (metric_ref, middle_ref), refs = refs[:2], refs[2:]
    if has_start:
        refs = refs[1:]
    out_ref, split_ref, in_ref, la_ref, lb_ref, result_ref, in_sems, out_sems = refs
    buffers, block, _ = in_ref.shape
    piece, width = right_a_refs[0].shape
    height = trailing_ref.shape[0]
    pieces = order_ref.shape[0]
    rows = height // pieces
    sub = rows // block
    steps = height // block

    def window(ref, step, i):
        top = order_ref[step // sub] * rows + lax.rem(step, sub) * block
        left = cols_ref[i] * piece
        if piece % 128 == 0:
            left = pl.multiple_of(left, 128)
        return ref.at[pl.ds(pl.multiple_of(top, 8), block), pl.ds(left, piece)]

    def in_copies(step):
        slot = lax.rem(step, buffers)
        out = []
        for i in range(count):
            target = in_ref.at[slot, :, pl.ds(i * piece, piece)]
            out.append(pltpu.make_async_copy(window(trailing_ref, step, i), target, in_sems.at[slot, i]))
        where = pl.ds(pl.multiple_of(step * block, 8), block)
        out.append(pltpu.make_async_copy(left_a_ref.at[where, :], la_ref.at[slot], in_sems.at[slot, count]))
        out.append(pltpu.make_async_copy(left_b_ref.at[where, :], lb_ref.at[slot], in_sems.at[slot, count + 1]))
        return out

    def out_copies(step):
        slot = lax.rem(step, buffers)
        out = []
        for i in range(count):
            source = result_ref.at[slot, :, pl.ds(i * piece, piece)]
            out.append(pltpu.make_async_copy(source, window(out_ref, step, i), out_sems.at[slot, i]))
        return out

    for step in range(buffers - 1):
        for copy in in_copies(jnp.int32(step)):
            copy.start()
    dims = ((1,), (0,))
    metric = split(metric_ref[...])
    middle = split(middle_ref[...])
    for i in range(count):
        basis = split(right_a_refs[i][...])
        prods = split(right_b_refs[i][...])
        first = contract_split(prods, metric, dims) - contract_split(basis, middle, dims)
        second = contract_split(basis, metric, dims)
        high, low = split(jnp.concatenate([first + first, second + second], axis=1))
        where = pl.ds(i * piece, piece)
        split_ref[where, : 2 * width] = high
        split_ref[where, 2 * width : 4 * width] = low
        split_ref[where, 4 * width :] = high

    def body(step, carry):
        @pl.when(step + buffers - 1 < steps)
        def _():
            for copy in in_copies(step + buffers - 1):
                copy.start()

        for copy in in_copies(step):
            copy.wait()

        @pl.when(step >= buffers)
        def _():
            for copy in out_copies(step - buffers):
                copy.wait()

        slot = lax.rem(step, buffers)
        high, low = split(jnp.concatenate([la_ref[slot], lb_ref[slot]], axis=1))
        left = jnp.concatenate([high, high, low], axis=1)
        change = contract(left, split_ref[...], ((1,), (1,)))
        result_ref[slot] = in_ref[slot] - change
        for copy in out_copies(step):
            copy.start()
        return carry

    lax.fori_loop(0, steps, body, 0)
    for step in range(max(steps - buffers, 0), steps):
        for copy in out_copies(jnp.int32(step)):
            copy.wait()


def update(trailing, left_a, left_b, right_a, right_b, metric, middle, columns, order, start):
    height, depth = trailing.shape
    count = len(right_a)
    piece, width = right_a[0].shape
    _, block = blocking(height // order.shape[0], count)
    smem = pl.BlockSpec(memory_space=pltpu.SMEM)
    vmem = pl.BlockSpec(memory_space=pltpu.VMEM)
    hbm = pl.BlockSpec(memory_space=pl.ANY)
    args = [columns, order, trailing, left_a, left_b, *right_a, *right_b, metric, middle]
    in_specs = [smem, smem, hbm, hbm, hbm] + [vmem] * (2 * count + 2)
    aliases = {}
    if start is not None:
        aliases = {len(args): 0}
        args.append(start)
        in_specs.append(hbm)
    return pl.pallas_call(
        functools.partial(update_kernel, count, start is not None),
        in_specs=in_specs,
        out_specs=hbm,
        out_shape=jax.ShapeDtypeStruct((height, depth), F32),
        input_output_aliases=aliases,
        scratch_shapes=[
            pltpu.VMEM((count * piece, 6 * width), BF16),
            pltpu.VMEM((BUFFERS, block, count * piece), F32),
            pltpu.VMEM((BUFFERS, block, width), F32),
            pltpu.VMEM((BUFFERS, block, width), F32),
            pltpu.VMEM((BUFFERS, block, count * piece), F32),
            pltpu.SemaphoreType.DMA((BUFFERS, count + 2)),
            pltpu.SemaphoreType.DMA((BUFFERS, count)),
        ],
        compiler_params=pltpu.CompilerParams(vmem_limit_bytes=VMEM_LIMIT),
        name="update",
    )(*args)


def bits_of(size):
    return size.bit_length() - 1


def swap(block, axis, mask):
    size = lax.axis_size(axis)
    return lax.ppermute(block, axis, [(i, i ^ mask) for i in range(size)])


def sum_over_all(block):
    for axis in ("row", "col"):
        for bit in range(bits_of(lax.axis_size(axis))):
            other = swap(block, axis, 1 << bit)
            block = block + other
    return block


def stage_masks(count, stage):
    if stage == count - 1:
        return 1, 1
    return 1 << (stage + 1), 1 << (count - 1 - stage)


def stage_swap(block, axis, stage):
    size = lax.axis_size(axis)
    masks = stage_masks(bits_of(size), stage)
    return lax.ppermute(block, axis, [(i, i ^ masks[i & 1]) for i in range(size)])


def gather_masks(count, odd, stages):
    if stages == 0:
        return [0]
    mask = stage_masks(count, stages - 1)[odd]
    own = gather_masks(count, odd, stages - 1)
    other = gather_masks(count, odd ^ (mask & 1), stages - 1)
    return own + [mask ^ m for m in other]


def gather_over(block, axis):
    for stage in range(bits_of(lax.axis_size(axis))):
        other = stage_swap(block, axis, stage)
        block = jnp.concatenate([block, other])
    return block


def scatter_sum_over(block, axis):
    for stage in reversed(range(bits_of(lax.axis_size(axis)))):
        half = block.shape[0] // 2
        other = stage_swap(block[half:], axis, stage)
        block = block[:half] + other
    return block


def by_parity(index, even, odd):
    return jnp.where(index & 1 == 0, jnp.array(even, jnp.int32), jnp.array(odd, jnp.int32))


def rotate_right(index, size):
    return (index >> 1) | ((index & 1) * (size >> 1))


def rotate_left(index, size):
    return ((index << 1) & (size - 1)) | (index >> (bits_of(size) - 1))


def column_pieces(block):
    row_devices = lax.axis_size("row")
    col_devices = lax.axis_size("col")
    per_owner = col_devices // row_devices
    received = []
    for turn in range(row_devices):
        perm = []
        for r in range(row_devices):
            for c in range(col_devices):
                target_row = r ^ rotate_right(c % row_devices, row_devices) ^ turn
                target_col = per_owner * r + c // row_devices
                perm.append((r * col_devices + c, target_row * col_devices + target_col))
        received.append(lax.ppermute(block, ("row", "col"), perm))
    return received


def in_index_order(received, mask):
    count = bits_of(len(received))
    shape = received[0].shape
    pieces = jnp.stack(received).reshape((2,) * count + shape)
    for bit in range(count):
        pieces = jnp.where((mask >> bit) & 1 == 0, pieces, jnp.flip(pieces, count - 1 - bit))
    pieces = pieces.reshape((len(received),) + shape)
    order = [rotate_right(i, len(received)) for i in range(len(received))]
    return [jnp.concatenate([pieces[i] for i in order])]


def groups_of(groups, count):
    if count == sum(len(group) for group in groups):
        return groups
    return (tuple(range(count)),)


def on_device(trailing, panel_block):
    row_devices = lax.axis_size("row")
    col_devices = lax.axis_size("col")
    row = lax.axis_index("row")
    column = lax.axis_index("col")
    rows, width = panel_block.shape
    mask = row ^ (column // (col_devices // row_devices))
    count = bits_of(col_devices)
    order = column ^ by_parity(column, *[gather_masks(count, odd, count) for odd in (0, 1)])
    narrow = rows % 128 != 0

    gram_one = sum_over_all(matmul(panel_block.T, panel_block))
    upper_one, inverse_one = factor(gram_one)
    panel_rows = gather_over(panel_block, "col")
    panel_cols = column_pieces(panel_block)
    if narrow:
        panel_cols = in_index_order(panel_cols, mask)
    pieces = len(panel_cols)
    columns = [jnp.zeros((1,), jnp.int32) if narrow else rotate_left(mask ^ i, pieces)[None] for i in range(pieces)]

    def pick(group, blocks):
        return [blocks[i] for i in group], jnp.concatenate([columns[i] for i in group])

    first_cols = [matmul(block, inverse_one.T) for block in panel_cols]
    own = matmul(panel_block, inverse_one.T)
    gram_two = matmul(own.T, own)
    partial = None
    for group in groups_of(PRODUCT_GROUPS, pieces):
        blocks, cols = pick(group, first_cols)
        partial = product(trailing, blocks, cols, order, partial)
    first_rows = matmul(panel_rows, inverse_one.T)
    inner = jnp.dot(first_rows.T, partial, preferred_element_type=F32, precision=lax.Precision.HIGH)
    sums = sum_over_all(jnp.concatenate([inner, gram_two]))
    inner, gram_two = sums[:width], sums[width:]
    mine = scatter_sum_over(partial, "col")
    product_cols = column_pieces(mine)
    if narrow:
        product_cols = in_index_order(product_cols, mask)
    product_rows = gather_over(mine, "col")

    upper_two, inverse_two = factor(gram_two)
    r_factor = matmul(upper_two, upper_one)
    metric = matmul(inverse_two.T, inverse_two)
    middle = matmul(matmul(metric, inner), metric)
    middle = middle + middle.T
    trailing_out = None
    for group in groups_of(UPDATE_GROUPS, pieces):
        right_a, cols = pick(group, first_cols)
        right_b, cols = pick(group, product_cols)
        trailing_out = update(
            trailing, first_rows, product_rows, right_a, right_b, metric, middle, cols, order, trailing_out
        )
    return (trailing_out, r_factor, upper_one)


def solution(mesh):
    in_specs = (P("row", "col"), P(("row", "col"), None))
    out_specs = (P("row", "col"), P(), P())

    return jax.shard_map(
        on_device, mesh=mesh, in_specs=in_specs, out_specs=out_specs, check_vma=False
    )
```

time: 788 us -> 220 us (0.28)
  waiting for transfers between devices: 594 us -> 46.5 us
  matrix products: 120 us -> 17.7 us
  Pallas kernels: 0 us -> 82.9 us
  starting transfers between devices: 0.99 us -> 55.7 us
  other arithmetic: 53.9 us -> 7.87 us
  between operations: 14.3 us -> 1.22 us
    psum x5 -> x0, waiting for transfers between devices: 488 us -> none  [the longest x1 127 us: on_device(): gram_one = lax.psum(matmul(panel_block.T, panel_block), ('row', 'col'))]
    dot_general x7 -> x13, matrix products: 119 us -> 17.7 us  [the longest x12 15.4 us: matmul(): return jnp.dot(first, second, preferred_element_type=F32, precision=HIGHEST)]
    pallas_call x0 -> x6, Pallas kernels: none -> 82.9 us  [the longest x2 43.2 us: update(): pl.pallas_call(functools.partial(update_kernel, count, start is not None)...]
    all_gather x2 -> x0, waiting for transfers between devices: 62.4 us -> none  [the longest x1 31.3 us: on_device(): basis_block = lax.all_gather(ortho_basis, 'col', axis=0, tiled=True)]
    ppermute x0 -> x27, starting transfers between devices: none -> 55.7 us  [the longest x8 28.5 us: column_pieces(): received.append(lax.ppermute(block, ('row', 'col'), perm))]
    ppermute x0 -> x27, waiting for transfers between devices: none -> 46.5 us  [the longest x9 24.6 us: stage_swap(): lax.ppermute(block, axis, [(i, i ^ masks[i & 1]) for i in range(size)])]
    another operation x9 -> x0, other arithmetic: 45.1 us -> none  [the longest x3 12.4 us: on_device(): low_one = jnp.linalg.cholesky(gram_one)]
    reduce_scatter x1 -> x0, waiting for transfers between devices: 43.2 us -> none  [on_device(): lax.psum_scatter(matmul(trailing, basis_cols), 'col', scatter_dimension=0...]
  transfers between devices with their start and end apart: 8 -> 27, of which waited for: 8 -> 13; matrix products, arithmetic and copies ran while one was open for 0% -> 11% of each run, Pallas kernels for 0% -> 24%
where the time goes in v1:
time: 220 us; the launch traced here: 216 us
  Pallas kernels  82.9 us (38%)
  starting transfers between devices  55.7 us (25%)
  waiting for transfers between devices  46.5 us (21%)
  matrix products  17.7 us (8%)
  other arithmetic  7.87 us (4%)
  local copies, waits for them, and re-layouts  3.81 us (2%)
    pallas_call x2, Pallas kernels, update(): pl.pallas_call(functools.partial(update_kernel, count, start is not None)...  43.2 us
    ppermute x8, starting transfers between devices, column_pieces(): received.append(lax.ppermute(block, ('row', 'col'), perm))  28.5 us
    pallas_call x2, Pallas kernels, product(): pl.pallas_call(functools.partial(product_kernel, count, start is not None...  26.5 us
    ppermute x9, waiting for transfers between devices, stage_swap(): lax.ppermute(block, axis, [(i, i ^ masks[i & 1]) for i in range(size)])  24.6 us
    ppermute x10, waiting for transfers between devices, swap(): return lax.ppermute(block, axis, [(i, i ^ mask) for i in range(size)])  21.9 us
    dot_general x12, matrix products, matmul(): return jnp.dot(first, second, preferred_element_type=F32, precision=HIGHEST)  15.4 us
    ppermute x10, starting transfers between devices, swap(): return lax.ppermute(block, axis, [(i, i ^ mask) for i in range(size)])  14.4 us
    pallas_call x2, Pallas kernels, factor(): pl.pallas_call(factor_kernel, out_shape=[jax.ShapeDtypeStruct(gram.shape,...  13.2 us
  transfers between devices with their start and end apart: 27, of which 13 were waited for; matrix products, arithmetic and copies ran while one was open for 11% of the time, Pallas kernels for 24%

profile of v1, /device:TPU:0, one launch (start us, length us, event | category | flops | bytes accessed | tf_op | source)
XLA Modules:
  0.0 215.7 jit_solution(3782429281651281255)
XLA Ops:
  2.4 3.1 %collective-permute-start.3 = (f32[128,128]{1,0:T(8,128)S(1)}, f32[128,128]{1,0:T(8,128)S(1)}, u32[]{:S(2)}, u32[]{:S(2)}) collective-permute-start(f32[128,128]{1,0:T(8,128)S(1)} %fusion.13), channel_id=1, source_target_pairs={{0,8},{8,0},{16,24},{24,16},{1,9},{9,1},{17,25},{25,17},{2,10},{10... | collective-permute-start | bytes 196616 | tf_op jit(solution)/shard_map/ppermute | solution.py:324
  5.5 2.2 %collective-permute-done.3 = f32[128,128]{1,0:T(8,128)S(1)} collective-permute-done((f32[128,128]{1,0:T(8,128)S(1)}, f32[128,128]{1,0:T(8,128)S(1)}, u32[]{:S(2)}, u32[]{:S(2)}) %collective-permute-start.3) | collective-permute-done | bytes 65568 | tf_op jit(solution)/shard_map/ppermute | solution.py:324
  7.8 3.1 %collective-permute-start.4 = (f32[128,128]{1,0:T(8,128)S(1)}, f32[128,128]{1,0:T(8,128)S(1)}, u32[]{:S(2)}, u32[]{:S(2)}) collective-permute-start(f32[128,128]{1,0:T(8,128)S(1)} %add.43), channel_id=1, source_target_pairs={{0,16},{8,24},{16,0},{24,8},{1,17},{9,25},{17,1},{25,9},{2,18},{10... | collective-permute-start | bytes 196616 | tf_op jit(solution)/shard_map/ppermute | solution.py:324
  10.9 2.2 %collective-permute-done.4 = f32[128,128]{1,0:T(8,128)S(1)} collective-permute-done((f32[128,128]{1,0:T(8,128)S(1)}, f32[128,128]{1,0:T(8,128)S(1)}, u32[]{:S(2)}, u32[]{:S(2)}) %collective-permute-start.4) | collective-permute-done | bytes 65568 | tf_op jit(solution)/shard_map/ppermute | solution.py:324
  13.2 3.8 %collective-permute-start.10 = (f32[640,128]{1,0:T(8,128)}, f32[640,128]{1,0:T(8,128)S(1)}, u32[]{:S(2)}, u32[]{:S(2)}) collective-permute-start(f32[640,128]{1,0:T(8,128)} %param.5), channel_id=1, source_target_pairs={{0,8},{1,24},{2,0},{3,16},{4,9},{5,25},{6,1},{7,17},{8,2},{9,18},{... | collective-permute-start | bytes 983048 | tf_op jit(solution)/shard_map/ppermute | solution.py:395
  18.7 7.7 %collective-permute-start.8 = (f32[640,128]{1,0:T(8,128)}, f32[640,128]{1,0:T(8,128)S(1)}, u32[]{:S(2)}, u32[]{:S(2)}) collective-permute-start(f32[640,128]{1,0:T(8,128)} %param.5), channel_id=1, source_target_pairs={{0,24},{1,8},{2,16},{3,0},{4,25},{5,9},{6,17},{7,1},{8,18},{9,2},{... | collective-permute-start | bytes 983048 | tf_op jit(solution)/shard_map/ppermute | solution.py:395
  26.4 3.1 %collective-permute-start.11 = (f32[640,128]{1,0:T(8,128)}, f32[640,128]{1,0:T(8,128)S(1)}, u32[]{:S(2)}, u32[]{:S(2)}) collective-permute-start(f32[640,128]{1,0:T(8,128)} %param.5), channel_id=1, source_target_pairs={{0,16},{1,0},{2,24},{3,8},{4,17},{5,1},{6,25},{7,9},{8,26},{9,10},... | collective-permute-start | bytes 983048 | tf_op jit(solution)/shard_map/ppermute | solution.py:395
  29.6 2.7 %collective-permute-start.6 = (f32[128,128]{1,0:T(8,128)S(1)}, f32[128,128]{1,0:T(8,128)S(1)}, u32[]{:S(2)}, u32[]{:S(2)}) collective-permute-start(f32[128,128]{1,0:T(8,128)S(1)} %add.45), channel_id=1, source_target_pairs={{0,2},{1,3},{2,0},{3,1},{4,6},{5,7},{6,4},{7,5},{8,10},{9,11},{10,... | collective-permute-start | bytes 196616 | tf_op jit(solution)/shard_map/ppermute | solution.py:324
  33.5 3.0 %collective-permute-done.6 = f32[128,128]{1,0:T(8,128)S(1)} collective-permute-done((f32[128,128]{1,0:T(8,128)S(1)}, f32[128,128]{1,0:T(8,128)S(1)}, u32[]{:S(2)}, u32[]{:S(2)}) %collective-permute-start.6) | collective-permute-done | bytes 65568 | tf_op jit(solution)/shard_map/ppermute | solution.py:324
  38.5 2.3 %collective-permute-done.7 = f32[128,128]{1,0:T(8,128)S(1)} collective-permute-done((f32[128,128]{1,0:T(8,128)S(1)}, f32[128,128]{1,0:T(8,128)S(1)}, u32[]{:S(2)}, u32[]{:S(2)}) %collective-permute-start.7) | collective-permute-done | bytes 65568 | tf_op jit(solution)/shard_map/ppermute | solution.py:324
  41.4 6.6 %factor.2 = (f32[128,128]{1,0:T(8,128)}, f32[128,128]{1,0:T(8,128)}) custom-call(f32[128,128]{1,0:T(8,128)} %add.47.gram_ref), custom_call_target="tpu_custom_call" | custom-call | tf_op jit(solution)/shard_map/factor/pallas_call | solution.py:71
  54.0 17.7 %product.2.refs_4_ = f32[5120,128]{1,0:T(8,128)} custom-call(s32[3]{0:T(128)} %pad_add_fusion.1.refs_0_, s32[8]{0:T(128)} %fusion.10.refs_1_, f32[5120,2560]{1,0:T(8,128)} %refs_2_.7, f32[640,128]{1,0:T(8,128)} %convolution_bitcast_fusion.2.refs_3_.refs_5_, f32[640,128]{1,0:T(8,128)} %convolution_bitcast_fusion.1.refs_4_.refs_6_, ...), custom_call_target="tpu_custom_call" | custom-call | tf_op jit(solution)/shard_map/product/pallas_call | solution.py:177
  72.9 8.8 %product.3 = f32[5120,128]{1,0:T(8,128)} custom-call(s32[1]{0:T(128)} %bitcast.1.refs_0_, s32[8]{0:T(128)} %fusion.10.refs_1_, f32[5120,2560]{1,0:T(8,128)} %refs_2_.7, f32[640,128]{1,0:T(8,128)} %convolution_bitcast_fusion.3.refs_3_.refs_6_, f32[5120,128]{1,0:T(8,128)} %product.2.refs_4_), custom_call_target="tpu_custom_call" | custom-call | tf_op jit(solution)/shard_map/product/pallas_call | solution.py:177
  83.4 3.8 %collective-permute-start = (f32[640,128]{1,0:T(8,128)S(1)}, f32[640,128]{1,0:T(8,128)S(1)}, u32[]{:S(2)}, u32[]{:S(2)}) collective-permute-start(f32[640,128]{1,0:T(8,128)S(1)} %copy-done.2), channel_id=1, source_target_pairs={{0,2},{1,5},{2,0},{3,7},{4,6},{5,1},{6,4},{7,3},{8,10},{9,13},{10,... | collective-permute-start | bytes 983048 | tf_op jit(solution)/shard_map/ppermute | solution.py:344
  87.1 5.1 %collective-permute-done = f32[640,128]{1,0:T(8,128)S(1)} collective-permute-done((f32[640,128]{1,0:T(8,128)S(1)}, f32[640,128]{1,0:T(8,128)S(1)}, u32[]{:S(2)}, u32[]{:S(2)}) %collective-permute-start) | collective-permute-done | bytes 327712 | tf_op jit(solution)/shard_map/ppermute | solution.py:344
  92.2 2.6 %collective-permute-start.1 = (f32[1280,128]{1,0:T(8,128)S(1)}, f32[1280,128]{1,0:T(8,128)S(1)}, u32[]{:S(2)}, u32[]{:S(2)}) collective-permute-start(f32[1280,128]{1,0:T(8,128)S(1)} %pad_maximum_fusion.3), channel_id=1, source_target_pairs={{0,4},{1,3},{2,6},{3,1},{4,0},{5,7},{6,2},{7,5},{8,12},{9,11},{10,... | collective-permute-start | bytes 1966088 | tf_op jit(solution)/shard_map/ppermute | solution.py:344
  95.1 8.2 %collective-permute-done.1 = f32[1280,128]{1,0:T(8,128)S(1)} collective-permute-done((f32[1280,128]{1,0:T(8,128)S(1)}, f32[1280,128]{1,0:T(8,128)S(1)}, u32[]{:S(2)}, u32[]{:S(2)}) %collective-permute-start.1) | collective-permute-done | bytes 655392 | tf_op jit(solution)/shard_map/ppermute | solution.py:344
  104.0 6.4 %collective-permute-done.13 = f32[1280,128]{1,0:T(8,128)S(1)} collective-permute-done((f32[1280,128]{1,0:T(8,128)S(1)}, f32[1280,128]{1,0:T(8,128)S(1)}, u32[]{:S(2)}, u32[]{:S(2)}) %collective-permute-start.13) | collective-permute-done | bytes 655392 | tf_op jit(solution)/shard_map/ppermute | solution.py:344
  110.5 2.1 collective-permute-start.14
  113.1 2.3 %fusion.refs_3_ = f32[5120,128]{1,0:T(8,128)S(1)} fusion(f32[128,128]{1,0:T(8,128)S(1)} %copy-done.3, f32[2560,128]{1,0:T(8,128)S(1)} %collective-permute-done.2, f32[1280,128]{1,0:T(8,128)S(1)} %collective-permute-done.1, f32[640,128]{1,0:T(8,128)S(1)} %collective-permute-done, f32[640,128]{1,0:T(8,128)S(1)} %copy-done.2), kind=kOutput, calls=%fused_computation | convolution fusion | flops 1008599040 | bytes 5308416 | tf_op jit(solution)/shard_map/dot_general | solution.py:21
  115.4 2.2 %collective-permute-done.14 = f32[640,128]{1,0:T(8,128)S(1)} collective-permute-done((f32[640,128]{1,0:T(8,128)S(1)}, f32[640,128]{1,0:T(8,128)S(1)}, u32[]{:S(2)}, u32[]{:S(2)}) %collective-permute-start.14) | collective-permute-done | bytes 327712 | tf_op jit(solution)/shard_map/ppermute | solution.py:344
  119.8 2.3 %fusion.14 = f32[128,128]{1,0:T(8,128)S(1)} fusion(f32[5120,128]{1,0:T(8,128)S(1)} %fusion.refs_3_, f32[5120,128]{1,0:T(8,128)S(1)} %copy-done.1), kind=kOutput, calls=%fused_computation.32 | convolution fusion | flops 503316480 | bytes 5308416 | tf_op jit(solution)/shard_map/dot_general | solution.py:447
  122.2 2.7 %collective-permute-done.15 = f32[640,128]{1,0:T(8,128)S(1)} collective-permute-done((f32[640,128]{1,0:T(8,128)S(1)}, f32[640,128]{1,0:T(8,128)S(1)}, u32[]{:S(2)}, u32[]{:S(2)}) %collective-permute-start.15) | collective-permute-done | bytes 327712 | tf_op jit(solution)/shard_map/ppermute | solution.py:344
  124.9 2.1 collective-permute-start.16
  127.5 6.5 %collective-permute-done.21 = f32[256,128]{1,0:T(8,128)S(1)} collective-permute-done((f32[256,128]{1,0:T(8,128)S(1)}, f32[256,128]{1,0:T(8,128)S(1)}, u32[]{:S(2)}, u32[]{:S(2)}) %collective-permute-start.21) | collective-permute-done | bytes 131104 | tf_op jit(solution)/shard_map/ppermute | solution.py:324
  136.8 4.2 %collective-permute-done.23 = f32[256,128]{1,0:T(8,128)S(1)} collective-permute-done((f32[256,128]{1,0:T(8,128)S(1)}, f32[256,128]{1,0:T(8,128)S(1)}, u32[]{:S(2)}, u32[]{:S(2)}) %collective-permute-start.23) | collective-permute-done | bytes 131104 | tf_op jit(solution)/shard_map/ppermute | solution.py:324
  141.0 2.1 collective-permute-start.24
  148.9 6.0 %collective-permute-start.19 = (f32[640,128]{1,0:T(8,128)S(1)}, f32[640,128]{1,0:T(8,128)S(1)}, u32[]{:S(2)}, u32[]{:S(2)}) collective-permute-start(f32[640,128]{1,0:T(8,128)S(1)} %slice_add_fusion.2), channel_id=1, source_target_pairs={{0,24},{1,8},{2,16},{3,0},{4,25},{5,9},{6,17},{7,1},{8,18},{9,2},{... | collective-permute-start | bytes 983048 | tf_op jit(solution)/shard_map/ppermute | solution.py:395
  155.0 2.8 %collective-permute-start.18 = (f32[640,128]{1,0:T(8,128)S(1)}, f32[640,128]{1,0:T(8,128)S(1)}, u32[]{:S(2)}, u32[]{:S(2)}) collective-permute-start(f32[640,128]{1,0:T(8,128)S(1)} %slice_add_fusion.2), channel_id=1, source_target_pairs={{0,16},{1,0},{2,24},{3,8},{4,17},{5,1},{6,25},{7,9},{8,26},{9,10},... | collective-permute-start | bytes 983048 | tf_op jit(solution)/shard_map/ppermute | solution.py:395
  158.5 6.6 %factor.3 = (f32[128,128]{1,0:T(8,128)}, f32[128,128]{1,0:T(8,128)}) custom-call(f32[128,128]{1,0:T(8,128)} %slice.38.gram_ref), custom_call_target="tpu_custom_call" | custom-call | tf_op jit(solution)/shard_map/factor/pallas_call | solution.py:71
  170.8 21.6 %update.2.refs_11_ = f32[5120,2560]{1,0:T(8,128)} custom-call(s32[2]{0:T(128)} %pad_add_fusion.2.refs_0_, s32[8]{0:T(128)} %fusion.10.refs_1_, f32[5120,2560]{1,0:T(8,128)} %refs_2_.7, f32[5120,128]{1,0:T(8,128)} %copy-done, f32[5120,128]{1,0:T(8,128)} %pad_maximum_fusion.refs_4_, f32[640,128]{1,0:T(8,128)} %convolution_bitcast_fusion.2.refs_3_.refs_5_, ...), custom_call_target="tpu_custom_call" | custom-call | tf_op jit(solution)/shard_map/update/pallas_call | solution.py:298
  193.9 21.6 %update.3 = f32[5120,2560]{1,0:T(8,128)} custom-call(s32[2]{0:T(128)} %pad_add_fusion.refs_0_, s32[8]{0:T(128)} %fusion.10.refs_1_, f32[5120,2560]{1,0:T(8,128)} %refs_2_.7, f32[5120,128]{1,0:T(8,128)} %copy-done, f32[5120,128]{1,0:T(8,128)} %pad_maximum_fusion.refs_4_, f32[640,128]{1,0:T(8,128)} %convolution_bitcast_fusion.refs_5_, ...), custom_call_target="tpu_custom_call", output_to_operand_aliasing={{}: (11, {})} | custom-call | tf_op jit(solution)/shard_map/update/pallas_call | solution.py:298
  (86 shorter events, 36.9 us)
Async XLA Ops:
  2.4 5.4 %collective-permute-start.3 = (f32[128,128]{1,0:T(8,128)S(1)}, f32[128,128]{1,0:T(8,128)S(1)}, u32[]{:S(2)}, u32[]{:S(2)}) collective-permute-start(f32[128,128]{1,0:T(8,128)S(1)} %fusion.13), channel_id=1, source_target_pairs={{0,8},{8,0},{16,24},{24,16},{1,9},{9,1},{17,25},{25,17},{2,10},{10... | collective-permute-start | bytes 196616 | tf_op jit(solution)/shard_map/ppermute | solution.py:324
  7.8 5.3 %collective-permute-start.4 = (f32[128,128]{1,0:T(8,128)S(1)}, f32[128,128]{1,0:T(8,128)S(1)}, u32[]{:S(2)}, u32[]{:S(2)}) collective-permute-start(f32[128,128]{1,0:T(8,128)S(1)} %add.43), channel_id=1, source_target_pairs={{0,16},{8,24},{16,0},{24,8},{1,17},{9,25},{17,1},{25,9},{2,18},{10... | collective-permute-start | bytes 196616 | tf_op jit(solution)/shard_map/ppermute | solution.py:324
  13.1 16.4 %collective-permute-start.5 = (f32[128,128]{1,0:T(8,128)S(1)}, f32[128,128]{1,0:T(8,128)S(1)}, u32[]{:S(2)}, u32[]{:S(2)}) collective-permute-start(f32[128,128]{1,0:T(8,128)S(1)} %add.44), channel_id=1, source_target_pairs={{0,1},{1,0},{2,3},{3,2},{4,5},{5,4},{6,7},{7,6},{8,9},{9,8},{10,11... | collective-permute-start | bytes 196616 | tf_op jit(solution)/shard_map/ppermute | solution.py:324
  13.2 34.8 %collective-permute-start.10 = (f32[640,128]{1,0:T(8,128)}, f32[640,128]{1,0:T(8,128)S(1)}, u32[]{:S(2)}, u32[]{:S(2)}) collective-permute-start(f32[640,128]{1,0:T(8,128)} %param.5), channel_id=1, source_target_pairs={{0,8},{1,24},{2,0},{3,16},{4,9},{5,25},{6,1},{7,17},{8,2},{9,18},{... | collective-permute-start | bytes 983048 | tf_op jit(solution)/shard_map/ppermute | solution.py:395
  17.0 32.9 %collective-permute-start.9 = (f32[640,128]{1,0:T(8,128)}, f32[640,128]{1,0:T(8,128)S(1)}, u32[]{:S(2)}, u32[]{:S(2)}) collective-permute-start(f32[640,128]{1,0:T(8,128)} %param.5), channel_id=1, source_target_pairs={{0,0},{1,16},{2,8},{3,24},{4,1},{5,17},{6,9},{7,25},{8,10},{9,26},... | collective-permute-start | bytes 983048 | tf_op jit(solution)/shard_map/ppermute | solution.py:395
  18.7 53.0 %collective-permute-start.8 = (f32[640,128]{1,0:T(8,128)}, f32[640,128]{1,0:T(8,128)S(1)}, u32[]{:S(2)}, u32[]{:S(2)}) collective-permute-start(f32[640,128]{1,0:T(8,128)} %param.5), channel_id=1, source_target_pairs={{0,24},{1,8},{2,16},{3,0},{4,25},{5,9},{6,17},{7,1},{8,18},{9,2},{... | collective-permute-start | bytes 983048 | tf_op jit(solution)/shard_map/ppermute | solution.py:395
  26.4 25.6 %collective-permute-start.11 = (f32[640,128]{1,0:T(8,128)}, f32[640,128]{1,0:T(8,128)S(1)}, u32[]{:S(2)}, u32[]{:S(2)}) collective-permute-start(f32[640,128]{1,0:T(8,128)} %param.5), channel_id=1, source_target_pairs={{0,16},{1,0},{2,24},{3,8},{4,17},{5,1},{6,25},{7,9},{8,26},{9,10},... | collective-permute-start | bytes 983048 | tf_op jit(solution)/shard_map/ppermute | solution.py:395
  29.6 6.8 %collective-permute-start.6 = (f32[128,128]{1,0:T(8,128)S(1)}, f32[128,128]{1,0:T(8,128)S(1)}, u32[]{:S(2)}, u32[]{:S(2)}) collective-permute-start(f32[128,128]{1,0:T(8,128)S(1)} %add.45), channel_id=1, source_target_pairs={{0,2},{1,3},{2,0},{3,1},{4,6},{5,7},{6,4},{7,5},{8,10},{9,11},{10,... | collective-permute-start | bytes 196616 | tf_op jit(solution)/shard_map/ppermute | solution.py:324
  36.4 4.3 %collective-permute-start.7 = (f32[128,128]{1,0:T(8,128)S(1)}, f32[128,128]{1,0:T(8,128)S(1)}, u32[]{:S(2)}, u32[]{:S(2)}) collective-permute-start(f32[128,128]{1,0:T(8,128)S(1)} %add.46), channel_id=1, source_target_pairs={{0,4},{1,5},{2,6},{3,7},{4,0},{5,1},{6,2},{7,3},{8,12},{9,13},{10,... | collective-permute-start | bytes 196616 | tf_op jit(solution)/shard_map/ppermute | solution.py:324
  54.0 17.7 %copy-start.3 = (f32[128,128]{1,0:T(8,128)S(1)}, f32[128,128]{1,0:T(8,128)}, u32[]{:S(2)}) copy-start(f32[128,128]{1,0:T(8,128)} %get-tuple-element.7) | copy-start | bytes 196612
  72.9 10.5 %copy-start.2 = (f32[640,128]{1,0:T(8,128)S(1)}, f32[640,128]{1,0:T(8,128)}, u32[]{:S(2)}) copy-start(f32[640,128]{1,0:T(8,128)} %param.5) | copy-start | bytes 983044
  81.7 13.1 %copy-start.1 = (f32[5120,128]{1,0:T(8,128)S(1)}, f32[5120,128]{1,0:T(8,128)}, u32[]{:S(2)}) copy-start(f32[5120,128]{1,0:T(8,128)} %product.3) | copy-start | bytes 7864324
  83.3 11.5 %collective-permute-start.12 = (f32[2560,128]{1,0:T(8,128)S(1)}, f32[2560,128]{1,0:T(8,128)S(1)}, u32[]{:S(2)}, u32[]{:S(2)}) collective-permute-start(f32[2560,128]{1,0:T(8,128)S(1)} %slice.33), channel_id=1, source_target_pairs={{0,1},{1,0},{2,3},{3,2},{4,5},{5,4},{6,7},{7,6},{8,9},{9,8},{10,11... | collective-permute-start | bytes 3932168 | tf_op jit(solution)/shard_map/ppermute | solution.py:344
  83.4 8.8 %collective-permute-start = (f32[640,128]{1,0:T(8,128)S(1)}, f32[640,128]{1,0:T(8,128)S(1)}, u32[]{:S(2)}, u32[]{:S(2)}) collective-permute-start(f32[640,128]{1,0:T(8,128)S(1)} %copy-done.2), channel_id=1, source_target_pairs={{0,2},{1,5},{2,0},{3,7},{4,6},{5,1},{6,4},{7,3},{8,10},{9,13},{10,... | collective-permute-start | bytes 983048 | tf_op jit(solution)/shard_map/ppermute | solution.py:344
  92.2 11.1 %collective-permute-start.1 = (f32[1280,128]{1,0:T(8,128)S(1)}, f32[1280,128]{1,0:T(8,128)S(1)}, u32[]{:S(2)}, u32[]{:S(2)}) collective-permute-start(f32[1280,128]{1,0:T(8,128)S(1)} %pad_maximum_fusion.3), channel_id=1, source_target_pairs={{0,4},{1,3},{2,6},{3,1},{4,0},{5,7},{6,2},{7,5},{8,12},{9,11},{10,... | collective-permute-start | bytes 1966088 | tf_op jit(solution)/shard_map/ppermute | solution.py:344
  95.0 15.3 %collective-permute-start.13 = (f32[1280,128]{1,0:T(8,128)S(1)}, f32[1280,128]{1,0:T(8,128)S(1)}, u32[]{:S(2)}, u32[]{:S(2)}) collective-permute-start(f32[1280,128]{1,0:T(8,128)S(1)} %slice.35), channel_id=1, source_target_pairs={{0,4},{1,3},{2,6},{3,1},{4,0},{5,7},{6,2},{7,5},{8,12},{9,11},{10,... | collective-permute-start | bytes 1966088 | tf_op jit(solution)/shard_map/ppermute | solution.py:344
  103.5 9.6 %collective-permute-start.2 = (f32[2560,128]{1,0:T(8,128)S(1)}, f32[2560,128]{1,0:T(8,128)S(1)}, u32[]{:S(2)}, u32[]{:S(2)}) collective-permute-start(f32[2560,128]{1,0:T(8,128)S(1)} %pad_maximum_fusion.1), channel_id=1, source_target_pairs={{0,1},{1,0},{2,3},{3,2},{4,5},{5,4},{6,7},{7,6},{8,9},{9,8},{10,11... | collective-permute-start | bytes 3932168 | tf_op jit(solution)/shard_map/ppermute | solution.py:344
  110.5 7.1 %collective-permute-start.14 = (f32[640,128]{1,0:T(8,128)S(1)}, f32[640,128]{1,0:T(8,128)S(1)}, u32[]{:S(2)}, u32[]{:S(2)}) collective-permute-start(f32[640,128]{1,0:T(8,128)S(1)} %slice.37), channel_id=1, source_target_pairs={{0,2},{1,5},{2,0},{3,7},{4,6},{5,1},{6,4},{7,3},{8,10},{9,13},{10,... | collective-permute-start | bytes 983048 | tf_op jit(solution)/shard_map/ppermute | solution.py:344
  115.4 6.7 %copy-start = (f32[5120,128]{1,0:T(8,128)}, f32[5120,128]{1,0:T(8,128)S(1)}, u32[]{:S(2)}) copy-start(f32[5120,128]{1,0:T(8,128)S(1)} %fusion.refs_3_) | copy-start | bytes 7864324
  117.7 7.1 %collective-permute-start.15 = (f32[640,128]{1,0:T(8,128)S(1)}, f32[640,128]{1,0:T(8,128)S(1)}, u32[]{:S(2)}, u32[]{:S(2)}) collective-permute-start(f32[640,128]{1,0:T(8,128)S(1)} %slice_add_fusion.2), channel_id=1, source_target_pairs={{0,2},{1,5},{2,0},{3,7},{4,6},{5,1},{6,4},{7,3},{8,10},{9,13},{10,... | collective-permute-start | bytes 983048 | tf_op jit(solution)/shard_map/ppermute | solution.py:344
  122.1 5.0 %collective-permute-start.20 = (f32[256,128]{1,0:T(8,128)S(1)}, f32[256,128]{1,0:T(8,128)S(1)}, u32[]{:S(2)}, u32[]{:S(2)}) collective-permute-start(f32[256,128]{1,0:T(8,128)S(1)} %pad_maximum_fusion.5), channel_id=1, source_target_pairs={{0,8},{8,0},{16,24},{24,16},{1,9},{9,1},{17,25},{25,17},{2,10},{10... | collective-permute-start | bytes 393224 | tf_op jit(solution)/shard_map/ppermute | solution.py:324
  124.9 18.3 %collective-permute-start.16 = (f32[1280,128]{1,0:T(8,128)S(1)}, f32[1280,128]{1,0:T(8,128)S(1)}, u32[]{:S(2)}, u32[]{:S(2)}) collective-permute-start(f32[1280,128]{1,0:T(8,128)S(1)} %pad_maximum_fusion.4), channel_id=1, source_target_pairs={{0,4},{1,3},{2,6},{3,1},{4,0},{5,7},{6,2},{7,5},{8,12},{9,11},{10,... | collective-permute-start | bytes 1966088 | tf_op jit(solution)/shard_map/ppermute | solution.py:344
  127.1 40.3 %copy-start.7 = (f32[128,128]{1,0:T(8,128)S(1)}, f32[128,128]{1,0:T(8,128)}, u32[]{:S(2)}) copy-start(f32[128,128]{1,0:T(8,128)} %get-tuple-element.6) | copy-start | bytes 196612
  127.1 6.8 %collective-permute-start.21 = (f32[256,128]{1,0:T(8,128)S(1)}, f32[256,128]{1,0:T(8,128)S(1)}, u32[]{:S(2)}, u32[]{:S(2)}) collective-permute-start(f32[256,128]{1,0:T(8,128)S(1)} %fusion.12), channel_id=1, source_target_pairs={{0,16},{8,24},{16,0},{24,8},{1,17},{9,25},{17,1},{25,9},{2,18},{10... | collective-permute-start | bytes 393224 | tf_op jit(solution)/shard_map/ppermute | solution.py:324
  133.9 1.4 collective-permute-start.22
  135.4 5.6 %collective-permute-start.23 = (f32[256,128]{1,0:T(8,128)S(1)}, f32[256,128]{1,0:T(8,128)S(1)}, u32[]{:S(2)}, u32[]{:S(2)}) collective-permute-start(f32[256,128]{1,0:T(8,128)S(1)} %add.53), channel_id=1, source_target_pairs={{0,2},{1,3},{2,0},{3,1},{4,6},{5,7},{6,4},{7,5},{8,10},{9,11},{10,... | collective-permute-start | bytes 393224 | tf_op jit(solution)/shard_map/ppermute | solution.py:324
  141.0 14.0 %collective-permute-start.24 = (f32[256,128]{1,0:T(8,128)S(1)}, f32[256,128]{1,0:T(8,128)S(1)}, u32[]{:S(2)}, u32[]{:S(2)}) collective-permute-start(f32[256,128]{1,0:T(8,128)S(1)} %add.54), channel_id=1, source_target_pairs={{0,4},{1,5},{2,6},{3,7},{4,0},{5,1},{6,2},{7,3},{8,12},{9,13},{10,... | collective-permute-start | bytes 393224 | tf_op jit(solution)/shard_map/ppermute | solution.py:324
  144.3 24.8 %collective-permute-start.17 = (f32[2560,128]{1,0:T(8,128)}, f32[2560,128]{1,0:T(8,128)S(1)}, u32[]{:S(2)}, u32[]{:S(2)}) collective-permute-start(f32[2560,128]{1,0:T(8,128)} %pad_maximum_fusion.2), channel_id=1, source_target_pairs={{0,1},{1,0},{2,3},{3,2},{4,5},{5,4},{6,7},{7,6},{8,9},{9,8},{10,11... | collective-permute-start | bytes 3932168 | tf_op jit(solution)/shard_map/ppermute | solution.py:344
  145.6 25.2 %collective-permute-start.26 = (f32[640,128]{1,0:T(8,128)S(1)}, f32[640,128]{1,0:T(8,128)}, u32[]{:S(2)}, u32[]{:S(2)}) collective-permute-start(f32[640,128]{1,0:T(8,128)S(1)} %slice_add_fusion.2), channel_id=1, source_target_pairs={{0,8},{1,24},{2,0},{3,16},{4,9},{5,25},{6,1},{7,17},{8,2},{9,18},{... | collective-permute-start | bytes 983048 | tf_op jit(solution)/shard_map/ppermute | solution.py:395
  147.5 23.3 %collective-permute-start.25 = (f32[640,128]{1,0:T(8,128)S(1)}, f32[640,128]{1,0:T(8,128)}, u32[]{:S(2)}, u32[]{:S(2)}) collective-permute-start(f32[640,128]{1,0:T(8,128)S(1)} %slice_add_fusion.2), channel_id=1, source_target_pairs={{0,0},{1,16},{2,8},{3,24},{4,1},{5,17},{6,9},{7,25},{8,10},{9,26},... | collective-permute-start | bytes 983048 | tf_op jit(solution)/shard_map/ppermute | solution.py:395
  148.9 43.5 %collective-permute-start.19 = (f32[640,128]{1,0:T(8,128)S(1)}, f32[640,128]{1,0:T(8,128)S(1)}, u32[]{:S(2)}, u32[]{:S(2)}) collective-permute-start(f32[640,128]{1,0:T(8,128)S(1)} %slice_add_fusion.2), channel_id=1, source_target_pairs={{0,24},{1,8},{2,16},{3,0},{4,25},{5,9},{6,17},{7,1},{8,18},{9,2},{... | collective-permute-start | bytes 983048 | tf_op jit(solution)/shard_map/ppermute | solution.py:395
  155.0 37.5 %collective-permute-start.18 = (f32[640,128]{1,0:T(8,128)S(1)}, f32[640,128]{1,0:T(8,128)S(1)}, u32[]{:S(2)}, u32[]{:S(2)}) collective-permute-start(f32[640,128]{1,0:T(8,128)S(1)} %slice_add_fusion.2), channel_id=1, source_target_pairs={{0,16},{1,0},{2,24},{3,8},{4,17},{5,1},{6,25},{7,9},{8,26},{9,10},... | collective-permute-start | bytes 983048 | tf_op jit(solution)/shard_map/ppermute | solution.py:395
  (3 other events, 6.0 us)

commit v2 on v1

--- a/solution.py
+++ b/solution.py
@@ -192,6 +192,25 @@
     )(*args)
 
 
+def basis_kernel(count, *refs):
+    inverse = refs[0][...]
+    for source, target in zip(refs[1:count + 1], refs[count + 1:]):
+        target[...] = lax.dot_general(
+            source[...], inverse, (((1,), (1,)), ((), ())), precision=HIGHEST, preferred_element_type=F32
+        )
+
+
+def basis_pieces(panel_pieces, inverse):
+    count = len(panel_pieces)
+    if count == 1:
+        return [matmul(panel_pieces[0], inverse.T)]
+    return pl.pallas_call(
+        functools.partial(basis_kernel, count),
+        out_shape=[jax.ShapeDtypeStruct(piece.shape, F32) for piece in panel_pieces],
+        name="basis",
+    )(inverse, *panel_pieces)
+
+
 def update_kernel(count, has_start, *refs):
     (cols_ref, order_ref, trailing_ref, left_a_ref, left_b_ref), refs = refs[:5], refs[5:]
     right_a_refs, refs = refs[:count], refs[count:]
@@ -436,7 +455,9 @@
     def pick(group, blocks):
         return [blocks[i] for i in group], jnp.concatenate([columns[i] for i in group])
 
-    first_cols = [matmul(block, inverse_one.T) for block in panel_cols]
+    first_cols = []
+    for group in groups_of(PRODUCT_GROUPS, pieces):
+        first_cols += basis_pieces([panel_cols[i] for i in group], inverse_one)
     own = matmul(panel_block, inverse_one.T)
     gram_two = matmul(own.T, own)
     partial = None

time: 220 us -> 218 us (level)
  matrix products: 17.7 us -> 11.7 us
  Pallas kernels: 82.9 us -> 85.9 us
    dot_general x12 -> x9, matrix products: 15.4 us -> 9.45 us  [matmul(): return jnp.dot(first, second, preferred_element_type=F32, precision=HIGHEST)]
    pallas_call x0 -> x1, Pallas kernels: none -> 2.98 us  [basis_pieces(): pl.pallas_call(functools.partial(basis_kernel, count), out_shape=[jax.Sha...]
  transfers between devices with their start and end apart: 27 -> 27, of which waited for: 13 -> 13; matrix products, arithmetic and copies ran while one was open for 11% -> 8% of each run, Pallas kernels for 24% -> 26%
where the time goes in v2:
time: 218 us; the launch traced here: 214 us
  Pallas kernels  85.9 us (39%)
  starting transfers between devices  56.9 us (26%)
  waiting for transfers between devices  45.8 us (21%)
  matrix products  11.7 us (5%)
  other arithmetic  7.86 us (4%)
  local copies, waits for them, and re-layouts  4.74 us (2%)
    pallas_call x2, Pallas kernels, update(): pl.pallas_call(functools.partial(update_kernel, count, start is not None)...  43.2 us
    ppermute x8, starting transfers between devices, column_pieces(): received.append(lax.ppermute(block, ('row', 'col'), perm))  29 us
    pallas_call x2, Pallas kernels, product(): pl.pallas_call(functools.partial(product_kernel, count, start is not None...  26.5 us
    ppermute x9, waiting for transfers between devices, stage_swap(): lax.ppermute(block, axis, [(i, i ^ masks[i & 1]) for i in range(size)])  24.6 us
    ppermute x10, waiting for transfers between devices, swap(): return lax.ppermute(block, axis, [(i, i ^ mask) for i in range(size)])  21.2 us
    ppermute x10, starting transfers between devices, swap(): return lax.ppermute(block, axis, [(i, i ^ mask) for i in range(size)])  15 us
    pallas_call x2, Pallas kernels, factor(): pl.pallas_call(factor_kernel, out_shape=[jax.ShapeDtypeStruct(gram.shape,...  13.2 us
    ppermute x9, starting transfers between devices, stage_swap(): lax.ppermute(block, axis, [(i, i ^ masks[i & 1]) for i in range(size)])  12.8 us
  transfers between devices with their start and end apart: 27, of which 13 were waited for; matrix products, arithmetic and copies ran while one was open for 8% of the time, Pallas kernels for 26%

profile of v2, /device:TPU:0, one launch (start us, length us, event | category | flops | bytes accessed | tf_op | source)
XLA Modules:
  0.0 214.1 jit_solution(173193271309285690)
XLA Ops:
  2.4 3.1 %collective-permute-start.3 = (f32[128,128]{1,0:T(8,128)S(1)}, f32[128,128]{1,0:T(8,128)S(1)}, u32[]{:S(2)}, u32[]{:S(2)}) collective-permute-start(f32[128,128]{1,0:T(8,128)S(1)} %fusion.13), channel_id=1, source_target_pairs={{0,8},{8,0},{16,24},{24,16},{1,9},{9,1},{17,25},{25,17},{2,10},{10... | collective-permute-start | bytes 196616 | tf_op jit(solution)/shard_map/ppermute | solution.py:343
  5.5 2.2 %collective-permute-done.3 = f32[128,128]{1,0:T(8,128)S(1)} collective-permute-done((f32[128,128]{1,0:T(8,128)S(1)}, f32[128,128]{1,0:T(8,128)S(1)}, u32[]{:S(2)}, u32[]{:S(2)}) %collective-permute-start.3) | collective-permute-done | bytes 65568 | tf_op jit(solution)/shard_map/ppermute | solution.py:343
  7.8 3.1 %collective-permute-start.4 = (f32[128,128]{1,0:T(8,128)S(1)}, f32[128,128]{1,0:T(8,128)S(1)}, u32[]{:S(2)}, u32[]{:S(2)}) collective-permute-start(f32[128,128]{1,0:T(8,128)S(1)} %add.43), channel_id=1, source_target_pairs={{0,16},{8,24},{16,0},{24,8},{1,17},{9,25},{17,1},{25,9},{2,18},{10... | collective-permute-start | bytes 196616 | tf_op jit(solution)/shard_map/ppermute | solution.py:343
  10.9 2.2 %collective-permute-done.4 = f32[128,128]{1,0:T(8,128)S(1)} collective-permute-done((f32[128,128]{1,0:T(8,128)S(1)}, f32[128,128]{1,0:T(8,128)S(1)}, u32[]{:S(2)}, u32[]{:S(2)}) %collective-permute-start.4) | collective-permute-done | bytes 65568 | tf_op jit(solution)/shard_map/ppermute | solution.py:343
  13.2 3.8 %collective-permute-start.10 = (f32[640,128]{1,0:T(8,128)}, f32[640,128]{1,0:T(8,128)S(1)}, u32[]{:S(2)}, u32[]{:S(2)}) collective-permute-start(f32[640,128]{1,0:T(8,128)} %param.5), channel_id=1, source_target_pairs={{0,8},{1,24},{2,0},{3,16},{4,9},{5,25},{6,1},{7,17},{8,2},{9,18},{... | collective-permute-start | bytes 983048 | tf_op jit(solution)/shard_map/ppermute | solution.py:414
  18.7 7.7 %collective-permute-start.8 = (f32[640,128]{1,0:T(8,128)}, f32[640,128]{1,0:T(8,128)S(1)}, u32[]{:S(2)}, u32[]{:S(2)}) collective-permute-start(f32[640,128]{1,0:T(8,128)} %param.5), channel_id=1, source_target_pairs={{0,24},{1,8},{2,16},{3,0},{4,25},{5,9},{6,17},{7,1},{8,18},{9,2},{... | collective-permute-start | bytes 983048 | tf_op jit(solution)/shard_map/ppermute | solution.py:414
  26.4 3.1 %collective-permute-start.11 = (f32[640,128]{1,0:T(8,128)}, f32[640,128]{1,0:T(8,128)S(1)}, u32[]{:S(2)}, u32[]{:S(2)}) collective-permute-start(f32[640,128]{1,0:T(8,128)} %param.5), channel_id=1, source_target_pairs={{0,16},{1,0},{2,24},{3,8},{4,17},{5,1},{6,25},{7,9},{8,26},{9,10},... | collective-permute-start | bytes 983048 | tf_op jit(solution)/shard_map/ppermute | solution.py:414
  29.6 2.7 %collective-permute-start.6 = (f32[128,128]{1,0:T(8,128)S(1)}, f32[128,128]{1,0:T(8,128)S(1)}, u32[]{:S(2)}, u32[]{:S(2)}) collective-permute-start(f32[128,128]{1,0:T(8,128)S(1)} %add.45), channel_id=1, source_target_pairs={{0,2},{1,3},{2,0},{3,1},{4,6},{5,7},{6,4},{7,5},{8,10},{9,11},{10,... | collective-permute-start | bytes 196616 | tf_op jit(solution)/shard_map/ppermute | solution.py:343
  33.5 2.9 %collective-permute-done.6 = f32[128,128]{1,0:T(8,128)S(1)} collective-permute-done((f32[128,128]{1,0:T(8,128)S(1)}, f32[128,128]{1,0:T(8,128)S(1)}, u32[]{:S(2)}, u32[]{:S(2)}) %collective-permute-start.6) | collective-permute-done | bytes 65568 | tf_op jit(solution)/shard_map/ppermute | solution.py:343
  38.5 2.3 %collective-permute-done.7 = f32[128,128]{1,0:T(8,128)S(1)} collective-permute-done((f32[128,128]{1,0:T(8,128)S(1)}, f32[128,128]{1,0:T(8,128)S(1)}, u32[]{:S(2)}, u32[]{:S(2)}) %collective-permute-start.7) | collective-permute-done | bytes 65568 | tf_op jit(solution)/shard_map/ppermute | solution.py:343
  41.4 6.6 %factor.2 = (f32[128,128]{1,0:T(8,128)}, f32[128,128]{1,0:T(8,128)}) custom-call(f32[128,128]{1,0:T(8,128)} %add.47.gram_ref), custom_call_target="tpu_custom_call" | custom-call | tf_op jit(solution)/shard_map/factor/pallas_call | solution.py:71
  48.9 3.0 %basis.1 = (f32[640,128]{1,0:T(8,128)}, f32[640,128]{1,0:T(8,128)}, f32[640,128]{1,0:T(8,128)}) custom-call(f32[128,128]{1,0:T(8,128)} %get-tuple-element.10.refs_0_, f32[640,128]{1,0:T(8,128)} %copy-done.8, f32[640,128]{1,0:T(8,128)} %copy-done.7, f32[640,128]{1,0:T(8,128)} %copy-done.9), custom_call_target="tpu_custom_call" | custom-call | tf_op jit(solution)/shard_map/basis/pallas_call | solution.py:207
  51.9 17.7 %product.2.refs_4_ = f32[5120,128]{1,0:T(8,128)} custom-call(s32[3]{0:T(128)} %pad_add_fusion.1.refs_0_, s32[8]{0:T(128)} %fusion.10.refs_1_, f32[5120,2560]{1,0:T(8,128)} %refs_2_.7, f32[640,128]{1,0:T(8,128)} %get-tuple-element.11.refs_3_.refs_5_, f32[640,128]{1,0:T(8,128)} %get-tuple-element.12.refs_4_.refs_6_, f32[640,128]{1,0:T(8,128)} %get-tuple-element.13.refs_5_), custom_call_target="tpu_custom_call" | custom-call | tf_op jit(solution)/shard_map/product/pallas_call | solution.py:177
  70.8 8.8 %product.3 = f32[5120,128]{1,0:T(8,128)} custom-call(s32[1]{0:T(128)} %bitcast.1.refs_0_, s32[8]{0:T(128)} %fusion.10.refs_1_, f32[5120,2560]{1,0:T(8,128)} %refs_2_.7, f32[640,128]{1,0:T(8,128)} %convolution_bitcast_fusion.refs_3_.refs_6_, f32[5120,128]{1,0:T(8,128)} %product.2.refs_4_), custom_call_target="tpu_custom_call" | custom-call | tf_op jit(solution)/shard_map/product/pallas_call | solution.py:177
  81.3 3.8 %collective-permute-start = (f32[640,128]{1,0:T(8,128)S(1)}, f32[640,128]{1,0:T(8,128)S(1)}, u32[]{:S(2)}, u32[]{:S(2)}) collective-permute-start(f32[640,128]{1,0:T(8,128)S(1)} %copy-done.2), channel_id=1, source_target_pairs={{0,2},{1,5},{2,0},{3,7},{4,6},{5,1},{6,4},{7,3},{8,10},{9,13},{10,... | collective-permute-start | bytes 983048 | tf_op jit(solution)/shard_map/ppermute | solution.py:363
  85.1 5.1 %collective-permute-done = f32[640,128]{1,0:T(8,128)S(1)} collective-permute-done((f32[640,128]{1,0:T(8,128)S(1)}, f32[640,128]{1,0:T(8,128)S(1)}, u32[]{:S(2)}, u32[]{:S(2)}) %collective-permute-start) | collective-permute-done | bytes 327712 | tf_op jit(solution)/shard_map/ppermute | solution.py:363
  90.2 2.5 %collective-permute-start.1 = (f32[1280,128]{1,0:T(8,128)S(1)}, f32[1280,128]{1,0:T(8,128)S(1)}, u32[]{:S(2)}, u32[]{:S(2)}) collective-permute-start(f32[1280,128]{1,0:T(8,128)S(1)} %pad_maximum_fusion.3), channel_id=1, source_target_pairs={{0,4},{1,3},{2,6},{3,1},{4,0},{5,7},{6,2},{7,5},{8,12},{9,11},{10,... | collective-permute-start | bytes 1966088 | tf_op jit(solution)/shard_map/ppermute | solution.py:363
  93.1 8.2 %collective-permute-done.1 = f32[1280,128]{1,0:T(8,128)S(1)} collective-permute-done((f32[1280,128]{1,0:T(8,128)S(1)}, f32[1280,128]{1,0:T(8,128)S(1)}, u32[]{:S(2)}, u32[]{:S(2)}) %collective-permute-start.1) | collective-permute-done | bytes 655392 | tf_op jit(solution)/shard_map/ppermute | solution.py:363
  101.9 6.4 %collective-permute-done.13 = f32[1280,128]{1,0:T(8,128)S(1)} collective-permute-done((f32[1280,128]{1,0:T(8,128)S(1)}, f32[1280,128]{1,0:T(8,128)S(1)}, u32[]{:S(2)}, u32[]{:S(2)}) %collective-permute-start.13) | collective-permute-done | bytes 655392 | tf_op jit(solution)/shard_map/ppermute | solution.py:363
  111.0 2.3 %fusion.refs_3_ = f32[5120,128]{1,0:T(8,128)S(1)} fusion(f32[128,128]{1,0:T(8,128)S(1)} %copy-done.4, f32[2560,128]{1,0:T(8,128)S(1)} %collective-permute-done.2, f32[1280,128]{1,0:T(8,128)S(1)} %collective-permute-done.1, f32[640,128]{1,0:T(8,128)S(1)} %collective-permute-done, f32[640,128]{1,0:T(8,128)S(1)} %copy-done.2), kind=kOutput, calls=%fused_computation | convolution fusion | flops 1008599040 | bytes 5308416 | tf_op jit(solution)/shard_map/dot_general | solution.py:21
  113.3 2.2 %collective-permute-done.14 = f32[640,128]{1,0:T(8,128)S(1)} collective-permute-done((f32[640,128]{1,0:T(8,128)S(1)}, f32[640,128]{1,0:T(8,128)S(1)}, u32[]{:S(2)}, u32[]{:S(2)}) %collective-permute-start.14) | collective-permute-done | bytes 327712 | tf_op jit(solution)/shard_map/ppermute | solution.py:363
  117.7 2.3 %fusion.14 = f32[128,128]{1,0:T(8,128)S(1)} fusion(f32[5120,128]{1,0:T(8,128)S(1)} %fusion.refs_3_, f32[5120,128]{1,0:T(8,128)S(1)} %copy-done.1), kind=kOutput, calls=%fused_computation.29 | convolution fusion | flops 503316480 | bytes 5308416 | tf_op jit(solution)/shard_map/dot_general | solution.py:468
  120.1 2.7 %collective-permute-done.15 = f32[640,128]{1,0:T(8,128)S(1)} collective-permute-done((f32[640,128]{1,0:T(8,128)S(1)}, f32[640,128]{1,0:T(8,128)S(1)}, u32[]{:S(2)}, u32[]{:S(2)}) %collective-permute-start.15) | collective-permute-done | bytes 327712 | tf_op jit(solution)/shard_map/ppermute | solution.py:363
  122.8 2.1 collective-permute-start.16
  126.0 5.8 %collective-permute-done.21 = f32[256,128]{1,0:T(8,128)S(1)} collective-permute-done((f32[256,128]{1,0:T(8,128)S(1)}, f32[256,128]{1,0:T(8,128)S(1)}, u32[]{:S(2)}, u32[]{:S(2)}) %collective-permute-start.21) | collective-permute-done | bytes 131104 | tf_op jit(solution)/shard_map/ppermute | solution.py:343
  134.7 4.2 %collective-permute-done.23 = f32[256,128]{1,0:T(8,128)S(1)} collective-permute-done((f32[256,128]{1,0:T(8,128)S(1)}, f32[256,128]{1,0:T(8,128)S(1)}, u32[]{:S(2)}, u32[]{:S(2)}) %collective-permute-start.23) | collective-permute-done | bytes 131104 | tf_op jit(solution)/shard_map/ppermute | solution.py:343
  138.9 2.1 collective-permute-start.24
  146.8 6.1 %collective-permute-start.19 = (f32[640,128]{1,0:T(8,128)S(1)}, f32[640,128]{1,0:T(8,128)S(1)}, u32[]{:S(2)}, u32[]{:S(2)}) collective-permute-start(f32[640,128]{1,0:T(8,128)S(1)} %slice_add_fusion.2), channel_id=1, source_target_pairs={{0,24},{1,8},{2,16},{3,0},{4,25},{5,9},{6,17},{7,1},{8,18},{9,2},{... | collective-permute-start | bytes 983048 | tf_op jit(solution)/shard_map/ppermute | solution.py:414
  152.9 3.4 %collective-permute-start.18 = (f32[640,128]{1,0:T(8,128)S(1)}, f32[640,128]{1,0:T(8,128)S(1)}, u32[]{:S(2)}, u32[]{:S(2)}) collective-permute-start(f32[640,128]{1,0:T(8,128)S(1)} %slice_add_fusion.2), channel_id=1, source_target_pairs={{0,16},{1,0},{2,24},{3,8},{4,17},{5,1},{6,25},{7,9},{8,26},{9,10},... | collective-permute-start | bytes 983048 | tf_op jit(solution)/shard_map/ppermute | solution.py:414
  156.9 6.6 %factor.3 = (f32[128,128]{1,0:T(8,128)}, f32[128,128]{1,0:T(8,128)}) custom-call(f32[128,128]{1,0:T(8,128)} %slice.38.gram_ref), custom_call_target="tpu_custom_call" | custom-call | tf_op jit(solution)/shard_map/factor/pallas_call | solution.py:71
  169.2 21.6 %update.2.refs_11_ = f32[5120,2560]{1,0:T(8,128)} custom-call(s32[2]{0:T(128)} %pad_add_fusion.2.refs_0_, s32[8]{0:T(128)} %fusion.10.refs_1_, f32[5120,2560]{1,0:T(8,128)} %refs_2_.7, f32[5120,128]{1,0:T(8,128)} %copy-done, f32[5120,128]{1,0:T(8,128)} %pad_maximum_fusion.refs_4_, f32[640,128]{1,0:T(8,128)} %get-tuple-element.11.refs_3_.refs_5_, ...), custom_call_target="tpu_custom_call" | custom-call | tf_op jit(solution)/shard_map/update/pallas_call | solution.py:317
  192.3 21.6 %update.3 = f32[5120,2560]{1,0:T(8,128)} custom-call(s32[2]{0:T(128)} %pad_add_fusion.refs_0_, s32[8]{0:T(128)} %fusion.10.refs_1_, f32[5120,2560]{1,0:T(8,128)} %refs_2_.7, f32[5120,128]{1,0:T(8,128)} %copy-done, f32[5120,128]{1,0:T(8,128)} %pad_maximum_fusion.refs_4_, f32[640,128]{1,0:T(8,128)} %get-tuple-element.13.refs_5_, ...), custom_call_target="tpu_custom_call", output_to_operand_aliasing={{}: (11, {})} | custom-call | tf_op jit(solution)/shard_map/update/pallas_call | solution.py:317
  (90 shorter events, 34.6 us)
Async XLA Ops:
  2.4 5.4 %collective-permute-start.3 = (f32[128,128]{1,0:T(8,128)S(1)}, f32[128,128]{1,0:T(8,128)S(1)}, u32[]{:S(2)}, u32[]{:S(2)}) collective-permute-start(f32[128,128]{1,0:T(8,128)S(1)} %fusion.13), channel_id=1, source_target_pairs={{0,8},{8,0},{16,24},{24,16},{1,9},{9,1},{17,25},{25,17},{2,10},{10... | collective-permute-start | bytes 196616 | tf_op jit(solution)/shard_map/ppermute | solution.py:343
  7.8 5.3 %collective-permute-start.4 = (f32[128,128]{1,0:T(8,128)S(1)}, f32[128,128]{1,0:T(8,128)S(1)}, u32[]{:S(2)}, u32[]{:S(2)}) collective-permute-start(f32[128,128]{1,0:T(8,128)S(1)} %add.43), channel_id=1, source_target_pairs={{0,16},{8,24},{16,0},{24,8},{1,17},{9,25},{17,1},{25,9},{2,18},{10... | collective-permute-start | bytes 196616 | tf_op jit(solution)/shard_map/ppermute | solution.py:343
  13.1 16.4 %collective-permute-start.5 = (f32[128,128]{1,0:T(8,128)S(1)}, f32[128,128]{1,0:T(8,128)S(1)}, u32[]{:S(2)}, u32[]{:S(2)}) collective-permute-start(f32[128,128]{1,0:T(8,128)S(1)} %add.44), channel_id=1, source_target_pairs={{0,1},{1,0},{2,3},{3,2},{4,5},{5,4},{6,7},{7,6},{8,9},{9,8},{10,11... | collective-permute-start | bytes 196616 | tf_op jit(solution)/shard_map/ppermute | solution.py:343
  13.2 34.8 %collective-permute-start.10 = (f32[640,128]{1,0:T(8,128)}, f32[640,128]{1,0:T(8,128)S(1)}, u32[]{:S(2)}, u32[]{:S(2)}) collective-permute-start(f32[640,128]{1,0:T(8,128)} %param.5), channel_id=1, source_target_pairs={{0,8},{1,24},{2,0},{3,16},{4,9},{5,25},{6,1},{7,17},{8,2},{9,18},{... | collective-permute-start | bytes 983048 | tf_op jit(solution)/shard_map/ppermute | solution.py:414
  17.0 30.9 %collective-permute-start.9 = (f32[640,128]{1,0:T(8,128)}, f32[640,128]{1,0:T(8,128)S(1)}, u32[]{:S(2)}, u32[]{:S(2)}) collective-permute-start(f32[640,128]{1,0:T(8,128)} %param.5), channel_id=1, source_target_pairs={{0,0},{1,16},{2,8},{3,24},{4,1},{5,17},{6,9},{7,25},{8,10},{9,26},... | collective-permute-start | bytes 983048 | tf_op jit(solution)/shard_map/ppermute | solution.py:414
  18.7 50.9 %collective-permute-start.8 = (f32[640,128]{1,0:T(8,128)}, f32[640,128]{1,0:T(8,128)S(1)}, u32[]{:S(2)}, u32[]{:S(2)}) collective-permute-start(f32[640,128]{1,0:T(8,128)} %param.5), channel_id=1, source_target_pairs={{0,24},{1,8},{2,16},{3,0},{4,25},{5,9},{6,17},{7,1},{8,18},{9,2},{... | collective-permute-start | bytes 983048 | tf_op jit(solution)/shard_map/ppermute | solution.py:414
  26.4 21.6 %collective-permute-start.11 = (f32[640,128]{1,0:T(8,128)}, f32[640,128]{1,0:T(8,128)S(1)}, u32[]{:S(2)}, u32[]{:S(2)}) collective-permute-start(f32[640,128]{1,0:T(8,128)} %param.5), channel_id=1, source_target_pairs={{0,16},{1,0},{2,24},{3,8},{4,17},{5,1},{6,25},{7,9},{8,26},{9,10},... | collective-permute-start | bytes 983048 | tf_op jit(solution)/shard_map/ppermute | solution.py:414
  29.6 6.8 %collective-permute-start.6 = (f32[128,128]{1,0:T(8,128)S(1)}, f32[128,128]{1,0:T(8,128)S(1)}, u32[]{:S(2)}, u32[]{:S(2)}) collective-permute-start(f32[128,128]{1,0:T(8,128)S(1)} %add.45), channel_id=1, source_target_pairs={{0,2},{1,3},{2,0},{3,1},{4,6},{5,7},{6,4},{7,5},{8,10},{9,11},{10,... | collective-permute-start | bytes 196616 | tf_op jit(solution)/shard_map/ppermute | solution.py:343
  36.4 4.3 %collective-permute-start.7 = (f32[128,128]{1,0:T(8,128)S(1)}, f32[128,128]{1,0:T(8,128)S(1)}, u32[]{:S(2)}, u32[]{:S(2)}) collective-permute-start(f32[128,128]{1,0:T(8,128)S(1)} %add.46), channel_id=1, source_target_pairs={{0,4},{1,5},{2,6},{3,7},{4,0},{5,1},{6,2},{7,3},{8,12},{9,13},{10,... | collective-permute-start | bytes 196616 | tf_op jit(solution)/shard_map/ppermute | solution.py:343
  51.9 17.7 %copy-start.4 = (f32[128,128]{1,0:T(8,128)S(1)}, f32[128,128]{1,0:T(8,128)}, u32[]{:S(2)}) copy-start(f32[128,128]{1,0:T(8,128)} %get-tuple-element.10.refs_0_) | copy-start | bytes 196612
  70.8 10.5 %copy-start.2 = (f32[640,128]{1,0:T(8,128)S(1)}, f32[640,128]{1,0:T(8,128)}, u32[]{:S(2)}) copy-start(f32[640,128]{1,0:T(8,128)} %param.5) | copy-start | bytes 983044
  79.6 13.1 %copy-start.1 = (f32[5120,128]{1,0:T(8,128)S(1)}, f32[5120,128]{1,0:T(8,128)}, u32[]{:S(2)}) copy-start(f32[5120,128]{1,0:T(8,128)} %product.3) | copy-start | bytes 7864324
  81.2 11.5 %collective-permute-start.12 = (f32[2560,128]{1,0:T(8,128)S(1)}, f32[2560,128]{1,0:T(8,128)S(1)}, u32[]{:S(2)}, u32[]{:S(2)}) collective-permute-start(f32[2560,128]{1,0:T(8,128)S(1)} %slice.33), channel_id=1, source_target_pairs={{0,1},{1,0},{2,3},{3,2},{4,5},{5,4},{6,7},{7,6},{8,9},{9,8},{10,11... | collective-permute-start | bytes 3932168 | tf_op jit(solution)/shard_map/ppermute | solution.py:363
  81.3 8.8 %collective-permute-start = (f32[640,128]{1,0:T(8,128)S(1)}, f32[640,128]{1,0:T(8,128)S(1)}, u32[]{:S(2)}, u32[]{:S(2)}) collective-permute-start(f32[640,128]{1,0:T(8,128)S(1)} %copy-done.2), channel_id=1, source_target_pairs={{0,2},{1,5},{2,0},{3,7},{4,6},{5,1},{6,4},{7,3},{8,10},{9,13},{10,... | collective-permute-start | bytes 983048 | tf_op jit(solution)/shard_map/ppermute | solution.py:363
  90.2 11.1 %collective-permute-start.1 = (f32[1280,128]{1,0:T(8,128)S(1)}, f32[1280,128]{1,0:T(8,128)S(1)}, u32[]{:S(2)}, u32[]{:S(2)}) collective-permute-start(f32[1280,128]{1,0:T(8,128)S(1)} %pad_maximum_fusion.3), channel_id=1, source_target_pairs={{0,4},{1,3},{2,6},{3,1},{4,0},{5,7},{6,2},{7,5},{8,12},{9,11},{10,... | collective-permute-start | bytes 1966088 | tf_op jit(solution)/shard_map/ppermute | solution.py:363
  93.0 15.3 %collective-permute-start.13 = (f32[1280,128]{1,0:T(8,128)S(1)}, f32[1280,128]{1,0:T(8,128)S(1)}, u32[]{:S(2)}, u32[]{:S(2)}) collective-permute-start(f32[1280,128]{1,0:T(8,128)S(1)} %slice.35), channel_id=1, source_target_pairs={{0,4},{1,3},{2,6},{3,1},{4,0},{5,7},{6,2},{7,5},{8,12},{9,11},{10,... | collective-permute-start | bytes 1966088 | tf_op jit(solution)/shard_map/ppermute | solution.py:363
  101.4 9.6 %collective-permute-start.2 = (f32[2560,128]{1,0:T(8,128)S(1)}, f32[2560,128]{1,0:T(8,128)S(1)}, u32[]{:S(2)}, u32[]{:S(2)}) collective-permute-start(f32[2560,128]{1,0:T(8,128)S(1)} %pad_maximum_fusion.1), channel_id=1, source_target_pairs={{0,1},{1,0},{2,3},{3,2},{4,5},{5,4},{6,7},{7,6},{8,9},{9,8},{10,11... | collective-permute-start | bytes 3932168 | tf_op jit(solution)/shard_map/ppermute | solution.py:363
  108.4 7.1 %collective-permute-start.14 = (f32[640,128]{1,0:T(8,128)S(1)}, f32[640,128]{1,0:T(8,128)S(1)}, u32[]{:S(2)}, u32[]{:S(2)}) collective-permute-start(f32[640,128]{1,0:T(8,128)S(1)} %slice.37), channel_id=1, source_target_pairs={{0,2},{1,5},{2,0},{3,7},{4,6},{5,1},{6,4},{7,3},{8,10},{9,13},{10,... | collective-permute-start | bytes 983048 | tf_op jit(solution)/shard_map/ppermute | solution.py:363
  113.3 6.7 %copy-start = (f32[5120,128]{1,0:T(8,128)}, f32[5120,128]{1,0:T(8,128)S(1)}, u32[]{:S(2)}) copy-start(f32[5120,128]{1,0:T(8,128)S(1)} %fusion.refs_3_) | copy-start | bytes 7864324
  115.6 7.1 %collective-permute-start.15 = (f32[640,128]{1,0:T(8,128)S(1)}, f32[640,128]{1,0:T(8,128)S(1)}, u32[]{:S(2)}, u32[]{:S(2)}) collective-permute-start(f32[640,128]{1,0:T(8,128)S(1)} %slice_add_fusion.2), channel_id=1, source_target_pairs={{0,2},{1,5},{2,0},{3,7},{4,6},{5,1},{6,4},{7,3},{8,10},{9,13},{10,... | collective-permute-start | bytes 983048 | tf_op jit(solution)/shard_map/ppermute | solution.py:363
  120.0 5.0 %collective-permute-start.20 = (f32[256,128]{1,0:T(8,128)S(1)}, f32[256,128]{1,0:T(8,128)S(1)}, u32[]{:S(2)}, u32[]{:S(2)}) collective-permute-start(f32[256,128]{1,0:T(8,128)S(1)} %pad_maximum_fusion.5), channel_id=1, source_target_pairs={{0,8},{8,0},{16,24},{24,16},{1,9},{9,1},{17,25},{25,17},{2,10},{10... | collective-permute-start | bytes 393224 | tf_op jit(solution)/shard_map/ppermute | solution.py:343
  122.8 18.3 %collective-permute-start.16 = (f32[1280,128]{1,0:T(8,128)S(1)}, f32[1280,128]{1,0:T(8,128)S(1)}, u32[]{:S(2)}, u32[]{:S(2)}) collective-permute-start(f32[1280,128]{1,0:T(8,128)S(1)} %pad_maximum_fusion.4), channel_id=1, source_target_pairs={{0,4},{1,3},{2,6},{3,1},{4,0},{5,7},{6,2},{7,5},{8,12},{9,11},{10,... | collective-permute-start | bytes 1966088 | tf_op jit(solution)/shard_map/ppermute | solution.py:363
  125.1 40.8 %copy-start.10 = (f32[128,128]{1,0:T(8,128)S(1)}, f32[128,128]{1,0:T(8,128)}, u32[]{:S(2)}) copy-start(f32[128,128]{1,0:T(8,128)} %get-tuple-element.9) | copy-start | bytes 196612
  125.1 6.8 %collective-permute-start.21 = (f32[256,128]{1,0:T(8,128)S(1)}, f32[256,128]{1,0:T(8,128)S(1)}, u32[]{:S(2)}, u32[]{:S(2)}) collective-permute-start(f32[256,128]{1,0:T(8,128)S(1)} %fusion.12), channel_id=1, source_target_pairs={{0,16},{8,24},{16,0},{24,8},{1,17},{9,25},{17,1},{25,9},{2,18},{10... | collective-permute-start | bytes 393224 | tf_op jit(solution)/shard_map/ppermute | solution.py:343
  131.9 1.4 collective-permute-start.22
  133.3 5.6 %collective-permute-start.23 = (f32[256,128]{1,0:T(8,128)S(1)}, f32[256,128]{1,0:T(8,128)S(1)}, u32[]{:S(2)}, u32[]{:S(2)}) collective-permute-start(f32[256,128]{1,0:T(8,128)S(1)} %add.53), channel_id=1, source_target_pairs={{0,2},{1,3},{2,0},{3,1},{4,6},{5,7},{6,4},{7,5},{8,10},{9,11},{10,... | collective-permute-start | bytes 393224 | tf_op jit(solution)/shard_map/ppermute | solution.py:343
  138.9 13.9 %collective-permute-start.24 = (f32[256,128]{1,0:T(8,128)S(1)}, f32[256,128]{1,0:T(8,128)S(1)}, u32[]{:S(2)}, u32[]{:S(2)}) collective-permute-start(f32[256,128]{1,0:T(8,128)S(1)} %add.54), channel_id=1, source_target_pairs={{0,4},{1,5},{2,6},{3,7},{4,0},{5,1},{6,2},{7,3},{8,12},{9,13},{10,... | collective-permute-start | bytes 393224 | tf_op jit(solution)/shard_map/ppermute | solution.py:343
  142.2 25.3 %collective-permute-start.17 = (f32[2560,128]{1,0:T(8,128)}, f32[2560,128]{1,0:T(8,128)S(1)}, u32[]{:S(2)}, u32[]{:S(2)}) collective-permute-start(f32[2560,128]{1,0:T(8,128)} %pad_maximum_fusion.2), channel_id=1, source_target_pairs={{0,1},{1,0},{2,3},{3,2},{4,5},{5,4},{6,7},{7,6},{8,9},{9,8},{10,11... | collective-permute-start | bytes 3932168 | tf_op jit(solution)/shard_map/ppermute | solution.py:363
  143.5 25.7 %collective-permute-start.26 = (f32[640,128]{1,0:T(8,128)S(1)}, f32[640,128]{1,0:T(8,128)}, u32[]{:S(2)}, u32[]{:S(2)}) collective-permute-start(f32[640,128]{1,0:T(8,128)S(1)} %slice_add_fusion.2), channel_id=1, source_target_pairs={{0,8},{1,24},{2,0},{3,16},{4,9},{5,25},{6,1},{7,17},{8,2},{9,18},{... | collective-permute-start | bytes 983048 | tf_op jit(solution)/shard_map/ppermute | solution.py:414
  145.4 23.8 %collective-permute-start.25 = (f32[640,128]{1,0:T(8,128)S(1)}, f32[640,128]{1,0:T(8,128)}, u32[]{:S(2)}, u32[]{:S(2)}) collective-permute-start(f32[640,128]{1,0:T(8,128)S(1)} %slice_add_fusion.2), channel_id=1, source_target_pairs={{0,0},{1,16},{2,8},{3,24},{4,1},{5,17},{6,9},{7,25},{8,10},{9,26},... | collective-permute-start | bytes 983048 | tf_op jit(solution)/shard_map/ppermute | solution.py:414
  146.8 44.0 %collective-permute-start.19 = (f32[640,128]{1,0:T(8,128)S(1)}, f32[640,128]{1,0:T(8,128)S(1)}, u32[]{:S(2)}, u32[]{:S(2)}) collective-permute-start(f32[640,128]{1,0:T(8,128)S(1)} %slice_add_fusion.2), channel_id=1, source_target_pairs={{0,24},{1,8},{2,16},{3,0},{4,25},{5,9},{6,17},{7,1},{8,18},{9,2},{... | collective-permute-start | bytes 983048 | tf_op jit(solution)/shard_map/ppermute | solution.py:414
  152.9 38.0 %collective-permute-start.18 = (f32[640,128]{1,0:T(8,128)S(1)}, f32[640,128]{1,0:T(8,128)S(1)}, u32[]{:S(2)}, u32[]{:S(2)}) collective-permute-start(f32[640,128]{1,0:T(8,128)S(1)} %slice_add_fusion.2), channel_id=1, source_target_pairs={{0,16},{1,0},{2,24},{3,8},{4,17},{5,1},{6,25},{7,9},{8,26},{9,10},... | collective-permute-start | bytes 983048 | tf_op jit(solution)/shard_map/ppermute | solution.py:414
  (6 other events, 8.5 us)
